TPU v7x, 256 devices: a whole 4x4x8 slice. The times are simulated.
256 devices in a mesh: gx: 32 (over y, x, core), gy: 8 (over z).
Axes of the slice: x: 4, y: 4, z: 8, core: 2. Of those that a mesh axis runs over, the one named last changes fastest.
Arguments:
- labels: float32 [262144, 512], P(('gx', 'gy')), may hold values from -6 to 6
- point_order: int32 [256, 1024], P(('gx', 'gy')), may hold values from 0 to 1023, each once within a row
- leaf_inverse: float32 [262144, 1024], P(('gx', 'gy')), as said below
- leaf_basis: float32 [262144, 256], P(('gx', 'gy')), may hold values from -0.1875 to 0.1875
- couple_one: float32 [65536, 1024], P(('gx', 'gy'))
- transfer_one: float32 [65536, 256], P(('gx', 'gy')), may hold values from -0.1875 to 0.1875
- couple_two: float32 [16384, 1024], P(('gx', 'gy'))
- transfer_two: float32 [16384, 256], P(('gx', 'gy')), may hold values from -0.1875 to 0.1875
- couple_top: float32 [65536, 256], P(('gx', 'gy'))
Outputs:
- solution: float32 [262144, 512], P(('gx', 'gy'))
Inputs may be any that keep to these rules, and one draw needn't show every extreme that they name: Each row of point_order is a permutation of 0 to 1023. leaf_inverse, couple_one, couple_two and the top matrix assembled from couple_top are dense with a dominant diagonal.
All inputs are finite; a program needn't handle non-finite values.
Results may differ from a plain program's by a relative error of at most 0.00011.
Values sent between devices are 32-bit elements; how exact they have to be, the bound alone decides.
No kernel may reach another device: no remote copies, remote signals or barrier semaphores. Data moves between devices by JAX's collectives and lax.ppermute only.
A program may use at most 64 MiB of HBM per device.

v0:
```python
import jax
import jax.numpy as jnp
from jax import lax
from jax.experimental import pallas as pl
from jax.experimental.pallas import tpu as pltpu
from jax.sharding import PartitionSpec as P


ALL = ("gx", "gy")


def dot(left, right, left_dim=1, right_dim=0):
    return lax.dot_general(
        left, right, (((left_dim,), (right_dim,)), ((), ())), precision=lax.Precision.HIGH
    )


def line_shift(value, step, senders):
    pairs = [(i, i + step) for i in range(256) if i & 3 in senders]
    return lax.ppermute(value, ALL, pairs)


def ring_shift(value, step):
    return lax.ppermute(value, "gy", [(i, (i + step) % 8) for i in range(8)])


def other_core(value):
    return lax.ppermute(value, "gx", [(i, i ^ 1) for i in range(32)])


def join_partner(value, z, bit):
    other = lax.ppermute(value, "gy", [(i, i ^ 1 << bit) for i in range(8)])
    return jnp.where(z >> bit & 1 == 0, jnp.stack([value, other]), jnp.stack([other, value]))


def node_exchange(pieces):
    groups = [[16 * g + i for i in range(16)] for g in range(16)]
    return lax.all_to_all(pieces, ALL, 0, 0, axis_index_groups=groups)


def column(matrix, index):
    return lax.dynamic_slice(matrix, (0, (index & 3) * 256), (256, 256))


def node_gather(block, core):
    mine = lax.all_to_all(jnp.broadcast_to(block[None], (8,) + block.shape), "gy", 0, 0)
    theirs = other_core(mine)
    both = jnp.where(core == 0, jnp.stack([mine, theirs]), jnp.stack([theirs, mine]))
    return both.reshape((16 * block.shape[0], block.shape[1]))


def place_kernel(z_ref, *refs):
    pieces, (couple_ref, transfer_ref) = refs[:8], refs[8:]
    for k, s in enumerate(range(-3, 5)):
        row = pl.multiple_of(((z_ref[0] - s) & 7) * 64, 64)
        couple_ref[pl.ds(row, 64), :] = pieces[k][:, :1024]
        transfer_ref[pl.ds(row, 64), :] = pieces[k][:, 1024:]


def place_rows(pieces, z):
    return pl.pallas_call(
        place_kernel,
        out_shape=(
            jax.ShapeDtypeStruct((512, 1024), jnp.float32),
            jax.ShapeDtypeStruct((512, 256), jnp.float32),
        ),
        in_specs=[pl.BlockSpec(memory_space=pltpu.SMEM)]
        + [pl.BlockSpec(memory_space=pltpu.VMEM)] * 8,
        out_specs=(pl.BlockSpec(memory_space=pltpu.VMEM),) * 2,
    )(z.reshape(1), *pieces)


def per_device(
    labels,
    point_order,
    leaf_inverse,
    leaf_basis,
    couple_one,
    transfer_one,
    couple_two,
    transfer_two,
    couple_top,
):
    gx, z = lax.axis_index("gx"), lax.axis_index("gy")
    core, child, half = gx & 1, z & 3, z >> 2
    order_row = point_order[0]
    barrier = lax.optimization_barrier

    unorder = lambda rows: jnp.zeros_like(rows).at[order_row].set(rows, unique_indices=True)

    gains = dot(transfer_one, couple_one, 0, 0)
    ring = jnp.concatenate([couple_two, transfer_two], 1)
    gain_right = line_shift(column(gains, child + 3), 1, (0,))
    gain_left = line_shift(column(gains, child - 3), -1, (3,))
    ring_right, ring_left = ring_shift(ring, 1), ring_shift(ring, -1)
    rhs = labels[order_row]
    gain_right, gain_left, ring_right, ring_left, rhs = barrier(
        (gain_right, gain_left, ring_right, ring_left, rhs)
    )
    rings = {0: ring, 1: ring_right, -1: ring_left}

    gain_right = line_shift(column(gains, child + 2) + gain_right, 1, (0, 1))
    gain_left = line_shift(column(gains, child - 2) + gain_left, -1, (3, 2))
    ring_right, ring_left = ring_shift(ring_right, 1), ring_shift(ring_left, -1)
    solved = dot(leaf_inverse, rhs)
    gain_right, gain_left, ring_right, ring_left, solved = barrier(
        (gain_right, gain_left, ring_right, ring_left, solved)
    )
    rings |= {2: ring_right, -2: ring_left}

    gain_right = line_shift(column(gains, child + 1) + gain_right, 1, (0, 1, 2))
    gain_left = line_shift(column(gains, child - 1) + gain_left, -1, (3, 2, 1))
    ring_right, ring_left = ring_shift(ring_right, 1), ring_shift(ring_left, -1)
    proj = dot(leaf_basis, solved, 0, 0)
    block = jnp.concatenate([proj, transfer_one], 1)
    gain_right, gain_left, ring_right, ring_left, proj, block, leaf_inverse = barrier(
        (gain_right, gain_left, ring_right, ring_left, proj, block, leaf_inverse)
    )
    rings |= {3: ring_right, -3: ring_left}

    ring_right = ring_shift(ring_right, 1)
    gain_one = column(gains, child) + gain_right + gain_left
    partial = dot(proj, gain_one, 0, 1)
    parts = node_exchange(partial.reshape(16, 32, 256))
    right_one = line_shift(block, 1, (0, 1, 2))
    left_one = line_shift(block, -1, (3, 2, 1))
    back = dot(leaf_inverse, leaf_basis)
    back_out = unorder(back)
    solved_out = unorder(solved)
    parts, ring_right, right_one, left_one, back_out, solved_out = barrier(
        (parts, ring_right, right_one, left_one, back_out, solved_out)
    )
    rings |= {4: ring_right}

    right_two = line_shift(right_one, 1, (1, 2))
    left_two = line_shift(left_one, -1, (2, 1))
    couple_core, transfer_core = place_rows([rings[s] for s in range(-3, 5)], z)
    stack_mine = parts.reshape(4, 4, 32, 256).sum(1)
    stack_other = other_core(stack_mine)
    stack_two = jnp.where(
        core == 0,
        jnp.concatenate([stack_mine, stack_other], 1),
        jnp.concatenate([stack_other, stack_mine], 1),
    )
    stack_two = jnp.concatenate([stack_two[c] for c in range(4)], 1)
    solve_two = dot(stack_two, couple_core, 1, 1)
    far = lax.ppermute(
        jnp.where(half == 0, solve_two[:, 256:], solve_two[:, :256]),
        "gy",
        [(i, i ^ 4) for i in range(8)],
    )
    near = jnp.where(half == 0, solve_two[:, :256], solve_two[:, 256:])
    shares = jnp.where(half == 0, jnp.stack([near, far]), jnp.stack([far, near]))
    reduced = dot(solve_two, transfer_core)
    reduced = lax.dynamic_slice(reduced, (core * 32, 0), (32, 256)) + other_core(
        lax.dynamic_slice(reduced, ((1 - core) * 32, 0), (32, 256))
    )
    reduced_all = node_gather(reduced, core)
    reduced_all, right_two, left_two, shares = barrier((reduced_all, right_two, left_two, shares))

    right_three = line_shift(right_two, 1, (2,))
    left_three = line_shift(left_two, -1, (1,))
    shares = join_partner(shares, z, 0)
    top_partial = dot(couple_top, reduced_all, 1, 1).reshape(16, 16, 512)
    planes = [[i for i in range(32) if i % 2 == k] for k in range(2)]
    own_rows = lax.all_to_all(top_partial, "gx", 0, 0, axis_index_groups=planes).sum(0)
    own_rows, right_three, left_three, shares = barrier(
        (own_rows, right_three, left_three, shares)
    )

    shares = join_partner(shares, z, 1)
    block_two = node_gather(own_rows, core)

    couple_turned = jnp.concatenate([column(couple_one, child - s) for s in range(4)], 1)
    stack_one = jnp.concatenate(
        [block, right_one + left_three, right_two + left_two, right_three + left_one], 0
    )
    solve_lift = dot(couple_turned, stack_one)
    solve_one, lift_one = solve_lift[:, :512], solve_lift[:, 512:]

    transfer_other = other_core(transfer_core)
    transfer_all = jnp.where(
        core == 0,
        jnp.concatenate([transfer_core, transfer_other], 0),
        jnp.concatenate([transfer_other, transfer_core], 0),
    )
    lift_two = dot(lax.dynamic_slice(couple_core, (half * 256, 0), (256, 1024)), transfer_all)
    lift_both = dot(lift_one, lift_two)
    top_out = dot(back_out, lift_both)
    shares = shares.reshape(2, 2, 2, 2, 32, 256).transpose(3, 2, 0, 1, 4, 5)
    solve_two_own = shares.reshape(512, 256)
    known = solve_one - dot(lift_one, solve_two_own, 1, 1)
    base_out = solved_out - dot(back_out, known)
    return base_out - dot(top_out, block_two)


def solution(mesh):
    spec = P(ALL, None)
    return jax.shard_map(per_device, mesh=mesh, in_specs=(spec,) * 9, out_specs=spec, check_vma=False)
```

profile of v0, /device:TPU:1, one launch (start us, length us, event | category | flops | bytes accessed | tf_op | source)
XLA Modules:
  0.0 213.0 jit_solution(15734407811519700935)
XLA Ops:
  2.0 6.4 %collective-permute-start.3 = (f32[64,1280]{1,0:T(8,128)S(1)}, f32[64,1280]{1,0:T(8,128)}, u32[]{:S(2)}, u32[]{:S(2)}) collective-permute-start(f32[64,1280]{1,0:T(8,128)S(1)} %constant_dynamic-update-slice_fusion.refs_3_), channel_id=1, source_target_pairs={{0,7},{1,0},{2,1},{3,2},{4,3},{5,4},{6,5},{7,6},{8,15},{9,8},{10,9... | collective-permute-start | bytes 983048 | tf_op jit(solution)/shard_map/ppermute | solution.py:24
  8.4 1.9 fusion.49
  11.2 1.4 collective-permute-start.1
  12.6 2.0 collective-permute-start
  14.6 1.8 copy.12
  16.4 4.9 %gather_fusion = f32[1024,512]{1,0:T(8,128)} fusion(f32[1024,512]{1,0:T(8,128)S(1)} %copy-done, s32[1024]{0:T(1024)S(1)} %broadcast_clamp_fusion), kind=kCustom, calls=%fused_computation | custom fusion | bytes 4198400 | tf_op jit(solution)/shard_map/gather | solution.py:96
  23.1 4.0 %collective-permute-start.4 = (f32[256,256]{1,0:T(8,128)S(1)}, f32[256,256]{1,0:T(8,128)S(1)}, u32[]{:S(2)}, u32[]{:S(2)}) collective-permute-start(f32[256,256]{1,0:T(8,128)S(1)} %get-tuple-element.78), channel_id=1, source_target_pairs={{0,1},{1,2},{4,5},{5,6},{8,9},{9,10},{12,13},{13,14},{16,17},{17,1... | collective-permute-start | bytes 786440 | tf_op jit(solution)/shard_map/ppermute | solution.py:20
  27.1 2.1 %collective-permute-start.6 = (f32[64,1280]{1,0:T(8,128)}, f32[64,1280]{1,0:T(8,128)S(1)}, u32[]{:S(2)}, u32[]{:S(2)}) collective-permute-start(f32[64,1280]{1,0:T(8,128)} %collective-permute-done.2.refs_4_), channel_id=1, source_target_pairs={{0,1},{1,2},{2,3},{3,4},{4,5},{5,6},{6,7},{7,0},{8,9},{9,10},{10,1... | collective-permute-start | bytes 983048 | tf_op jit(solution)/shard_map/ppermute | solution.py:24
  29.8 9.4 %convolution_bitcast_fusion = f32[1024,512]{0,1:T(8,128)S(1)} fusion(f32[1024,512]{1,0:T(8,128)} %gather_fusion, f32[1024,1024]{1,0:T(8,128)} %param.11), kind=kOutput, calls=%fused_computation.12 | convolution fusion | flops 3221225472 | bytes 8388608 | tf_op jit(solution)/shard_map/dot_general | solution.py:13
  39.4 1.6 collective-permute-start.9
  41.0 4.0 %collective-permute-start.8 = (f32[256,256]{1,0:T(8,128)S(1)}, f32[256,256]{1,0:T(8,128)S(1)}, u32[]{:S(2)}, u32[]{:S(2)}) collective-permute-start(f32[256,256]{1,0:T(8,128)S(1)} %get-tuple-element.76), channel_id=1, source_target_pairs={{0,1},{1,2},{2,3},{4,5},{5,6},{6,7},{8,9},{9,10},{10,11},{12,13},{... | collective-permute-start | bytes 786440 | tf_op jit(solution)/shard_map/ppermute | solution.py:20
  45.0 1.4 collective-permute-start.10
  46.4 1.4 collective-permute-start.11
  49.8 5.2 %collective-permute-done.10.refs_6_ = f32[64,1280]{1,0:T(8,128)S(1)} collective-permute-done((f32[64,1280]{1,0:T(8,128)S(1)}, f32[64,1280]{1,0:T(8,128)S(1)}, u32[]{:S(2)}, u32[]{:S(2)}) %collective-permute-start.10) | collective-permute-done | bytes 327712 | tf_op jit(solution)/shard_map/ppermute | solution.py:24
  56.2 9.5 %all-to-all-start = ((f32[16,32,256]{2,1,0:T(8,128)}), f32[16,32,256]{2,1,0:T(8,128)}, u32[]{:S(2)}, u32[]{:S(2)}) async-start(f32[16,32,256]{2,1,0:T(8,128)} %bitcast.64), calls=%async_computation | async-start | bytes 1048576 | tf_op jit(solution)/shard_map/all_to_all | solution.py:38
  65.7 1.3 collective-permute-start.14
  67.0 5.1 %collective-permute-start.13 = (f32[256,768]{0,1:T(8,128)}, f32[256,768]{0,1:T(8,128)}, u32[]{:S(2)}, u32[]{:S(2)}) collective-permute-start(f32[256,768]{0,1:T(8,128)} %pad_maximum_fusion), channel_id=1, source_target_pairs={{0,1},{1,2},{2,3},{4,5},{5,6},{6,7},{8,9},{9,10},{10,11},{12,13},{... | collective-permute-start | bytes 2359304 | tf_op jit(solution)/shard_map/ppermute | solution.py:20
  72.1 2.9 %copy.13 = f32[1024,512]{1,0:T(8,128)} copy(f32[1024,512]{0,1:T(8,128)} %copy-done.1) | data formatting | bytes 4194304 | tf_op jit(solution)/shard_map/optimization_barrier | solution.py:106
  75.0 6.9 %scatter_custom_fusion.1 = f32[1024,512]{1,0:T(8,128)} fusion(s32[1024]{0:T(1024)S(1)} %bitcast.75, f32[1024,512]{1,0:T(8,128)} %copy.13, f32[]{:T(128)} %constant.15.clone.1), kind=kCustom, calls=%fused_computation.29 | custom fusion | bytes 2097664 | tf_op jit(solution)/shard_map/scatter | solution.py:89
  82.4 5.0 %fusion.50 = f32[1024,256]{1,0:T(8,128)} fusion(f32[1024,1024]{1,0:T(8,128)} %param.11, f32[1024,256]{1,0:T(8,128)S(1)} %copy-done.5), kind=kOutput, calls=%fused_computation.90 | convolution fusion | flops 1610612736 | bytes 6291456 | tf_op jit(solution)/shard_map/dot_general | solution.py:13
  87.4 5.5 %scatter_custom_fusion = f32[1024,256]{1,0:T(8,128)S(1)} fusion(s32[1024]{0:T(1024)S(1)} %bitcast.76, f32[1024,256]{1,0:T(8,128)} %fusion.50, f32[]{:T(128)} %constant.15.clone.1), kind=kCustom, calls=%fused_computation.40 | custom fusion | bytes 1049088 | tf_op jit(solution)/shard_map/scatter | solution.py:89
  92.9 8.5 %collective-permute-done.12.refs_7_ = f32[64,1280]{1,0:T(8,128)} collective-permute-done((f32[64,1280]{1,0:T(8,128)S(1)}, f32[64,1280]{1,0:T(8,128)}, u32[]{:S(2)}, u32[]{:S(2)}) %collective-permute-start.12) | collective-permute-done | bytes 327712 | tf_op jit(solution)/shard_map/ppermute | solution.py:24
  103.2 3.4 %shard_map.91 = (f32[512,1024]{1,0:T(8,128)}, f32[512,256]{1,0:T(8,128)}) custom-call(s32[1]{0:T(128)} %bitcast.10.z_ref, f32[64,1280]{1,0:T(8,128)} %copy-done.15, f32[64,1280]{1,0:T(8,128)} %copy-done.13, f32[64,1280]{1,0:T(8,128)} %collective-permute-done.3.refs_2_, f32[64,1280]{1,0:T(8,128)} %copy-done.7, f32[64,1280]{1,0:T(8,128)} %collective-permute-done.2.refs_4_, ...), custom_call_target="tpu_custom_call" | custom-call | tf_op jit(solution)/shard_map/pallas_call | solution.py:61
  106.6 2.7 %fusion.28 = f32[64,512]{1,0:T(8,128)S(1)} fusion(f32[512,1024]{1,0:T(8,128)} %get-tuple-element.60, f32[64,256]{1,0:T(8,128)S(1)} %get-tuple-element.84, f32[64,256]{1,0:T(8,128)S(1)} %get-tuple-element.85, f32[64,256]{1,0:T(8,128)S(1)} %get-tuple-element.86, f32[64,256]{1,0:T(8,128)S(1)} %get-tuple-element.83), kind=kOutput, calls=%fused_computation.44 | convolution fusion | flops 201523200 | bytes 2490368 | tf_op jit(solution)/shard_map/dot_general | solution.py:13
  111.7 7.6 %all-to-all-start.1 = ((f32[8,32,256]{2,1,0:T(8,128)}), f32[8,32,256]{2,1,0:T(8,128)S(1)}, u32[]{:S(2)}, u32[]{:S(2)}) async-start(f32[8,32,256]{2,1,0:T(8,128)} %broadcast_in_dim.10), calls=%async_computation.1 | async-start | bytes 524288 | tf_op jit(solution)/shard_map/all_to_all | solution.py:46
  119.3 1.6 collective-permute-start.18
  122.1 9.1 %all-to-all-done.1 = f32[8,32,256]{2,1,0:T(8,128)S(1)} async-done(((f32[8,32,256]{2,1,0:T(8,128)}), f32[8,32,256]{2,1,0:T(8,128)S(1)}, u32[]{:S(2)}, u32[]{:S(2)}) %all-to-all-start.1) | async-done | bytes 262176 | tf_op jit(solution)/shard_map/all_to_all | solution.py:46
  132.4 7.3 %collective-permute-done.20 = f32[64,256]{1,0:T(8,128)S(1)} collective-permute-done((f32[64,256]{1,0:T(8,128)S(1)}, f32[64,256]{1,0:T(8,128)S(1)}, u32[]{:S(2)}, u32[]{:S(2)}) %collective-permute-start.20) | collective-permute-done | bytes 65568 | tf_op jit(solution)/shard_map/ppermute | solution.py:147
  139.8 5.5 %collective-permute-done.19 = f32[256,768]{0,1:T(8,128)} collective-permute-done((f32[256,768]{0,1:T(8,128)}, f32[256,768]{0,1:T(8,128)}, u32[]{:S(2)}, u32[]{:S(2)}) %collective-permute-start.19) | collective-permute-done | bytes 786464 | tf_op jit(solution)/shard_map/ppermute | solution.py:20
  145.3 1.6 collective-permute-start.21
  148.1 2.6 %collective-permute-start.25 = (f32[512,256]{1,0:T(8,128)}, f32[512,256]{1,0:T(8,128)}, u32[]{:S(2)}, u32[]{:S(2)}) collective-permute-start(f32[512,256]{1,0:T(8,128)} %get-tuple-element.61), channel_id=1, source_target_pairs={{0,8},{8,0},{16,24},{24,16},{32,40},{40,32},{48,56},{56,48},{64,72... | collective-permute-start | bytes 1572872 | tf_op jit(solution)/shard_map/ppermute | solution.py:28
  150.7 2.2 %fusion.52 = f32[512,256]{0,1:T(8,128)} fusion(f32[512,256]{1,0:T(8,128)S(1)} %bitcast.62, f32[256,256]{1,0:T(8,128)} %param.17), kind=kOutput, calls=%fused_computation.92 | convolution fusion | flops 201326592 | bytes 1310720 | tf_op jit(solution)/shard_map/dot_general | solution.py:13
  152.9 6.8 %all-to-all-start.2 = ((f32[16,16,512]{2,1,0:T(8,128)}), f32[16,16,512]{2,1,0:T(8,128)}, u32[]{:S(2)}, u32[]{:S(2)}) async-start(f32[16,16,512]{2,1,0:T(8,128)} %bitcast.61), calls=%async_computation.2 | async-start | bytes 1048576 | tf_op jit(solution)/shard_map/all_to_all | solution.py:166
  159.7 5.3 %collective-permute-start.23 = (f32[2,64,256]{2,1,0:T(8,128)S(1)}, f32[2,64,256]{2,1,0:T(8,128)S(1)}, u32[]{:S(2)}, u32[]{:S(2)}) collective-permute-start(f32[2,64,256]{2,1,0:T(8,128)S(1)} %maximum_select_fusion.6), channel_id=1, source_target_pairs={{0,1},{1,0},{2,3},{3,2},{4,5},{5,4},{6,7},{7,6},{8,9},{9,8},{10,11... | collective-permute-start | bytes 393224 | tf_op jit(solution)/shard_map/ppermute | solution.py:32
  165.0 2.2 %constant_dynamic-slice_fusion.4 = (f32[256,256]{1,0:T(8,128)}, f32[256,256]{1,0:T(8,128)}, f32[256,256]{1,0:T(8,128)}, f32[256,256]{1,0:T(8,128)}) fusion(f32[256,1024]{1,0:T(8,128)} %param.13, s32[]{:T(128)S(6)} %select_n.130, s32[]{:T(128)S(6)} %select_n.129, s32[]{:T(128)S(6)} %select_n.126, s32[]{:T(128)S(6)} %select_n.128), kind=kLoop, calls=%fused_computation.81 | loop fusion | bytes 2097168 | tf_op jit(solution)/shard_map/dynamic_slice | solution.py:42
  167.2 3.2 %fusion.15 = f32[256,256]{1,0:T(8,128)} fusion(f32[512,256]{1,0:T(8,128)} %collective-permute-done.25, f32[512,256]{1,0:T(8,128)} %get-tuple-element.61, f32[512,1024]{1,0:T(8,128)} %get-tuple-element.60, s32[]{:T(128)S(6)} %select_n.147, pred[]{:T(512)S(6)} %eq.8), kind=kOutput, calls=%fused_computation.22 | convolution fusion | flops 403439616 | bytes 2359301 | tf_op jit(solution)/shard_map/dot_general | solution.py:13
  170.4 2.4 %add.109 = f32[256,768]{0,1:T(8,128)} add(f32[256,768]{0,1:T(8,128)} %collective-permute-done.18, f32[256,768]{0,1:T(8,128)} %collective-permute-done.19) | non-fusion elementwise | flops 196608 | bytes 2359296 | tf_op jit(solution)/shard_map/add | solution.py:176
  172.8 1.3 collective-permute-done.23
  175.2 2.4 %add.108 = f32[256,768]{0,1:T(8,128)} add(f32[256,768]{0,1:T(8,128)} %collective-permute-done.13, f32[256,768]{0,1:T(8,128)} %collective-permute-done.22) | non-fusion elementwise | flops 196608 | bytes 2359296 | tf_op jit(solution)/shard_map/add | solution.py:176
  177.6 2.4 %add.110 = f32[256,768]{0,1:T(8,128)} add(f32[256,768]{0,1:T(8,128)} %collective-permute-done.21, f32[256,768]{0,1:T(8,128)} %collective-permute-done.14) | non-fusion elementwise | flops 196608 | bytes 2359296 | tf_op jit(solution)/shard_map/add | solution.py:176
  180.7 4.0 %all-to-all-start.3 = ((f32[8,16,512]{2,1,0:T(8,128)}), f32[8,16,512]{2,1,0:T(8,128)}, u32[]{:S(2)}, u32[]{:S(2)}) async-start(f32[8,16,512]{2,1,0:T(8,128)} %broadcast_in_dim.11), calls=%async_computation.3 | async-start | bytes 524288 | tf_op jit(solution)/shard_map/all_to_all | solution.py:46
  184.8 2.2 %collective-permute-start.24 = (f32[2,2,64,256]{3,2,1,0:T(8,128)S(1)}, f32[2,2,64,256]{3,2,1,0:T(8,128)S(1)}, u32[]{:S(2)}, u32[]{:S(2)}) collective-permute-start(f32[2,2,64,256]{3,2,1,0:T(8,128)S(1)} %maximum_select_fusion.5), channel_id=1, source_target_pairs={{0,2},{1,3},{2,0},{3,1},{4,6},{5,7},{6,4},{7,5},{8,10},{9,11},{10,... | collective-permute-start | bytes 786440 | tf_op jit(solution)/shard_map/ppermute | solution.py:32
  187.0 3.7 %fusion = f32[256,768]{1,0:T(8,128)S(1)} fusion(f32[256,768]{0,1:T(8,128)} %add.110, f32[256,768]{0,1:T(8,128)} %add.109, f32[256,768]{0,1:T(8,128)} %add.108, f32[256,768]{0,1:T(8,128)} %pad_maximum_fusion, f32[256,256]{1,0:T(8,128)} %get-tuple-element.73, f32[256,256]{1,0:T(8,128)} %get-tuple-element.74, f32[256,256]{1,0:T(8,128)} %get-tuple-element.72, ...), kind=kOutput, calls=%fused_computation.3 | convolution fusion | flops 1211105280 | bytes 4980736 | tf_op jit(solution)/shard_map/dot_general | solution.py:13
  191.0 1.6 fusion.53
  192.6 11.3 %collective-permute-done.24 = f32[2,2,64,256]{3,2,1,0:T(8,128)S(1)} collective-permute-done((f32[2,2,64,256]{3,2,1,0:T(8,128)S(1)}, f32[2,2,64,256]{3,2,1,0:T(8,128)S(1)}, u32[]{:S(2)}, u32[]{:S(2)}) %collective-permute-start.24) | collective-permute-done | bytes 262176 | tf_op jit(solution)/shard_map/ppermute | solution.py:32
  205.4 1.8 collective-permute-start.26
  207.1 2.2 %fusion.24 = f32[1024,512]{1,0:T(8,128)S(1)} fusion(f32[1024,256]{1,0:T(8,128)S(1)} %scatter_custom_fusion, f32[256,512]{1,0:T(8,128)} %fusion.42, f32[256,768]{1,0:T(8,128)} %copy-done.6), kind=kOutput, calls=%fused_computation.33 | convolution fusion | flops 805437440 | bytes 4194304 | tf_op jit(solution)/shard_map/dot_general | solution.py:13
  210.5 2.5 %subtract_subtract_fusion = f32[1024,512]{1,0:T(8,128)} fusion(f32[1024,512]{1,0:T(8,128)S(1)} %copy-done.2, f32[1024,512]{1,0:T(8,128)S(1)} %fusion.24, f32[1024,256]{1,0:T(8,128)S(1)} %copy-done.3, f32[256,512]{1,0:T(8,128)S(1)} %bitcast.65), kind=kOutput, calls=%fused_computation.11 | convolution fusion | flops 806354944 | bytes 7864320 | tf_op jit(solution)/shard_map/dot_general | solution.py:13
  (98 shorter events, 21.6 us)
Async XLA Ops:
  0.0 16.4 %copy-start = (f32[1024,512]{1,0:T(8,128)S(1)}, f32[1024,512]{1,0:T(8,128)}, u32[]{:S(2)}) copy-start(f32[1024,512]{1,0:T(8,128)} %param.9) | copy-start | bytes 6291460
  0.0 14.6 %copy-start.17 = (s32[1,1024]{1,0:T(1,128)S(1)}, s32[1,1024]{1,0:T(1,128)}, u32[]{:S(2)}) copy-start(s32[1,1024]{1,0:T(1,128)} %param.10) | copy-start | bytes 12292
  2.0 19.2 %copy-start.7 = (f32[64,1280]{1,0:T(8,128)}, f32[64,1280]{1,0:T(8,128)S(1)}, u32[]{:S(2)}) copy-start(f32[64,1280]{1,0:T(8,128)S(1)} %constant_dynamic-update-slice_fusion.refs_3_) | copy-start | bytes 983044
  2.0 19.3 %collective-permute-start.3 = (f32[64,1280]{1,0:T(8,128)S(1)}, f32[64,1280]{1,0:T(8,128)}, u32[]{:S(2)}, u32[]{:S(2)}) collective-permute-start(f32[64,1280]{1,0:T(8,128)S(1)} %constant_dynamic-update-slice_fusion.refs_3_), channel_id=1, source_target_pairs={{0,7},{1,0},{2,1},{3,2},{4,3},{5,4},{6,5},{7,6},{8,15},{9,8},{10,9... | collective-permute-start | bytes 983048 | tf_op jit(solution)/shard_map/ppermute | solution.py:24
  8.4 12.9 %collective-permute-start.2 = (f32[64,1280]{1,0:T(8,128)S(1)}, f32[64,1280]{1,0:T(8,128)}, u32[]{:S(2)}, u32[]{:S(2)}) collective-permute-start(f32[64,1280]{1,0:T(8,128)S(1)} %constant_dynamic-update-slice_fusion.refs_3_), channel_id=1, source_target_pairs={{0,1},{1,2},{2,3},{3,4},{4,5},{5,6},{6,7},{7,0},{8,9},{9,10},{10,1... | collective-permute-start | bytes 983048 | tf_op jit(solution)/shard_map/ppermute | solution.py:24
  11.2 10.0 %collective-permute-start.1 = (f32[256,256]{1,0:T(8,128)}, f32[256,256]{1,0:T(8,128)}, u32[]{:S(2)}, u32[]{:S(2)}) collective-permute-start(f32[256,256]{1,0:T(8,128)} %get-tuple-element.79), channel_id=1, source_target_pairs={{3,2},{7,6},{11,10},{15,14},{19,18},{23,22},{27,26},{31,30},{35,34... | collective-permute-start | bytes 786440 | tf_op jit(solution)/shard_map/ppermute | solution.py:20
  12.6 8.7 %collective-permute-start = (f32[256,256]{1,0:T(8,128)}, f32[256,256]{1,0:T(8,128)}, u32[]{:S(2)}, u32[]{:S(2)}) collective-permute-start(f32[256,256]{1,0:T(8,128)} %get-tuple-element.80), channel_id=1, source_target_pairs={{0,1},{4,5},{8,9},{12,13},{16,17},{20,21},{24,25},{28,29},{32,33},... | collective-permute-start | bytes 786440 | tf_op jit(solution)/shard_map/ppermute | solution.py:20
  22.4 16.9 %collective-permute-start.5 = (f32[256,256]{1,0:T(8,128)S(1)}, f32[256,256]{1,0:T(8,128)S(1)}, u32[]{:S(2)}, u32[]{:S(2)}) collective-permute-start(f32[256,256]{1,0:T(8,128)S(1)} %get-tuple-element.77), channel_id=1, source_target_pairs={{2,1},{3,2},{6,5},{7,6},{10,9},{11,10},{14,13},{15,14},{18,17},{19... | collective-permute-start | bytes 786440 | tf_op jit(solution)/shard_map/ppermute | solution.py:20
  23.1 16.2 %collective-permute-start.4 = (f32[256,256]{1,0:T(8,128)S(1)}, f32[256,256]{1,0:T(8,128)S(1)}, u32[]{:S(2)}, u32[]{:S(2)}) collective-permute-start(f32[256,256]{1,0:T(8,128)S(1)} %get-tuple-element.78), channel_id=1, source_target_pairs={{0,1},{1,2},{4,5},{5,6},{8,9},{9,10},{12,13},{13,14},{16,17},{17,1... | collective-permute-start | bytes 786440 | tf_op jit(solution)/shard_map/ppermute | solution.py:20
  27.1 12.2 %collective-permute-start.6 = (f32[64,1280]{1,0:T(8,128)}, f32[64,1280]{1,0:T(8,128)S(1)}, u32[]{:S(2)}, u32[]{:S(2)}) collective-permute-start(f32[64,1280]{1,0:T(8,128)} %collective-permute-done.2.refs_4_), channel_id=1, source_target_pairs={{0,1},{1,2},{2,3},{3,4},{4,5},{5,6},{6,7},{7,0},{8,9},{9,10},{10,1... | collective-permute-start | bytes 983048 | tf_op jit(solution)/shard_map/ppermute | solution.py:24
  29.2 10.1 %collective-permute-start.7 = (f32[64,1280]{1,0:T(8,128)}, f32[64,1280]{1,0:T(8,128)S(1)}, u32[]{:S(2)}, u32[]{:S(2)}) collective-permute-start(f32[64,1280]{1,0:T(8,128)} %collective-permute-done.3.refs_2_), channel_id=1, source_target_pairs={{0,7},{1,0},{2,1},{3,2},{4,3},{5,4},{6,5},{7,6},{8,15},{9,8},{10,9... | collective-permute-start | bytes 983048 | tf_op jit(solution)/shard_map/ppermute | solution.py:24
  39.2 9.6 %copy-start.1 = (f32[1024,512]{0,1:T(8,128)}, f32[1024,512]{0,1:T(8,128)S(1)}, u32[]{:S(2)}) copy-start(f32[1024,512]{0,1:T(8,128)S(1)} %convolution_bitcast_fusion) | copy-start | bytes 6291460
  39.3 8.5 %copy-start.4 = (f32[1024,256]{1,0:T(8,128)S(1)}, f32[1024,256]{1,0:T(8,128)}, u32[]{:S(2)}) copy-start(f32[1024,256]{1,0:T(8,128)} %param.12) | copy-start | bytes 3145732
  39.3 9.5 %copy-start.12 = (f32[64,1280]{1,0:T(8,128)}, f32[64,1280]{1,0:T(8,128)S(1)}, u32[]{:S(2)}) copy-start(f32[64,1280]{1,0:T(8,128)S(1)} %collective-permute-done.6.refs_5_) | copy-start | bytes 983044
  39.3 9.5 %copy-start.13 = (f32[64,1280]{1,0:T(8,128)}, f32[64,1280]{1,0:T(8,128)S(1)}, u32[]{:S(2)}) copy-start(f32[64,1280]{1,0:T(8,128)S(1)} %collective-permute-done.7.refs_1_) | copy-start | bytes 983044
  39.4 9.4 %copy-start.8 = (f32[256,256]{0,1:T(8,128)S(1)}, f32[256,256]{0,1:T(8,128)}, u32[]{:S(2)}) copy-start(f32[256,256]{0,1:T(8,128)} %copy.12) | copy-start | bytes 786436
  39.4 10.4 %collective-permute-start.9 = (f32[256,256]{1,0:T(8,128)S(1)}, f32[256,256]{1,0:T(8,128)S(1)}, u32[]{:S(2)}, u32[]{:S(2)}) collective-permute-start(f32[256,256]{1,0:T(8,128)S(1)} %get-tuple-element.75), channel_id=1, source_target_pairs={{1,0},{2,1},{3,2},{5,4},{6,5},{7,6},{9,8},{10,9},{11,10},{13,12},{... | collective-permute-start | bytes 786440 | tf_op jit(solution)/shard_map/ppermute | solution.py:20
  41.0 8.8 %collective-permute-start.8 = (f32[256,256]{1,0:T(8,128)S(1)}, f32[256,256]{1,0:T(8,128)S(1)}, u32[]{:S(2)}, u32[]{:S(2)}) collective-permute-start(f32[256,256]{1,0:T(8,128)S(1)} %get-tuple-element.76), channel_id=1, source_target_pairs={{0,1},{1,2},{2,3},{4,5},{5,6},{6,7},{8,9},{9,10},{10,11},{12,13},{... | collective-permute-start | bytes 786440 | tf_op jit(solution)/shard_map/ppermute | solution.py:20
  45.0 10.0 %collective-permute-start.10 = (f32[64,1280]{1,0:T(8,128)S(1)}, f32[64,1280]{1,0:T(8,128)S(1)}, u32[]{:S(2)}, u32[]{:S(2)}) collective-permute-start(f32[64,1280]{1,0:T(8,128)S(1)} %collective-permute-done.6.refs_5_), channel_id=1, source_target_pairs={{0,1},{1,2},{2,3},{3,4},{4,5},{5,6},{6,7},{7,0},{8,9},{9,10},{10,1... | collective-permute-start | bytes 983048 | tf_op jit(solution)/shard_map/ppermute | solution.py:24
  46.4 8.6 %collective-permute-start.11 = (f32[64,1280]{1,0:T(8,128)S(1)}, f32[64,1280]{1,0:T(8,128)S(1)}, u32[]{:S(2)}, u32[]{:S(2)}) collective-permute-start(f32[64,1280]{1,0:T(8,128)S(1)} %collective-permute-done.7.refs_1_), channel_id=1, source_target_pairs={{0,7},{1,0},{2,1},{3,2},{4,3},{5,4},{6,5},{7,6},{8,15},{9,8},{10,9... | collective-permute-start | bytes 983048 | tf_op jit(solution)/shard_map/ppermute | solution.py:24
  55.0 26.9 %copy-start.14 = (f32[64,1280]{1,0:T(8,128)}, f32[64,1280]{1,0:T(8,128)S(1)}, u32[]{:S(2)}) copy-start(f32[64,1280]{1,0:T(8,128)S(1)} %collective-permute-done.10.refs_6_) | copy-start | bytes 983044
  56.2 45.2 %all-to-all-start = ((f32[16,32,256]{2,1,0:T(8,128)}), f32[16,32,256]{2,1,0:T(8,128)}, u32[]{:S(2)}, u32[]{:S(2)}) async-start(f32[16,32,256]{2,1,0:T(8,128)} %bitcast.64), calls=%async_computation | async-start | bytes 1048576 | tf_op jit(solution)/shard_map/all_to_all | solution.py:38
  65.7 35.7 %collective-permute-start.14 = (f32[256,768]{0,1:T(8,128)}, f32[256,768]{0,1:T(8,128)}, u32[]{:S(2)}, u32[]{:S(2)}) collective-permute-start(f32[256,768]{0,1:T(8,128)} %pad_maximum_fusion), channel_id=1, source_target_pairs={{1,0},{2,1},{3,2},{5,4},{6,5},{7,6},{9,8},{10,9},{11,10},{13,12},{... | collective-permute-start | bytes 2359304 | tf_op jit(solution)/shard_map/ppermute | solution.py:20
  67.0 34.4 %collective-permute-start.13 = (f32[256,768]{0,1:T(8,128)}, f32[256,768]{0,1:T(8,128)}, u32[]{:S(2)}, u32[]{:S(2)}) collective-permute-start(f32[256,768]{0,1:T(8,128)} %pad_maximum_fusion), channel_id=1, source_target_pairs={{0,1},{1,2},{2,3},{4,5},{5,6},{6,7},{8,9},{9,10},{10,11},{12,13},{... | collective-permute-start | bytes 2359304 | tf_op jit(solution)/shard_map/ppermute | solution.py:20
  75.0 7.4 %copy-start.5 = (f32[1024,256]{1,0:T(8,128)S(1)}, f32[1024,256]{1,0:T(8,128)}, u32[]{:S(2)}) copy-start(f32[1024,256]{1,0:T(8,128)} %param.12) | copy-start | bytes 3145732
  81.9 19.5 %collective-permute-start.12 = (f32[64,1280]{1,0:T(8,128)S(1)}, f32[64,1280]{1,0:T(8,128)}, u32[]{:S(2)}, u32[]{:S(2)}) collective-permute-start(f32[64,1280]{1,0:T(8,128)S(1)} %collective-permute-done.10.refs_6_), channel_id=1, source_target_pairs={{0,1},{1,2},{2,3},{3,4},{4,5},{5,6},{6,7},{7,0},{8,9},{9,10},{10,1... | collective-permute-start | bytes 983048 | tf_op jit(solution)/shard_map/ppermute | solution.py:24
  102.5 4.1 %collective-permute-start.15 = (f32[4,32,256]{2,1,0:T(8,128)S(1)}, f32[4,32,256]{2,1,0:T(8,128)S(1)}, u32[]{:S(2)}, u32[]{:S(2)}) collective-permute-start(f32[4,32,256]{2,1,0:T(8,128)S(1)} %bitcast_reduce_fusion), channel_id=1, source_target_pairs={{0,8},{8,0},{16,24},{24,16},{32,40},{40,32},{48,56},{56,48},{64,72... | collective-permute-start | bytes 393224 | tf_op jit(solution)/shard_map/ppermute | solution.py:28
  106.6 2.8 %copy-start.11 = (f32[512,256]{1,0:T(8,128)S(1)}, f32[512,256]{1,0:T(8,128)}, u32[]{:S(2)}) copy-start(f32[512,256]{1,0:T(8,128)} %get-tuple-element.61) | copy-start | bytes 1572868
  109.6 1.3 collective-permute-start.16
  111.7 19.6 %all-to-all-start.1 = ((f32[8,32,256]{2,1,0:T(8,128)}), f32[8,32,256]{2,1,0:T(8,128)S(1)}, u32[]{:S(2)}, u32[]{:S(2)}) async-start(f32[8,32,256]{2,1,0:T(8,128)} %broadcast_in_dim.10), calls=%async_computation.1 | async-start | bytes 524288 | tf_op jit(solution)/shard_map/all_to_all | solution.py:46
  119.3 20.5 %collective-permute-start.18 = (f32[256,768]{0,1:T(8,128)}, f32[256,768]{0,1:T(8,128)}, u32[]{:S(2)}, u32[]{:S(2)}) collective-permute-start(f32[256,768]{0,1:T(8,128)} %collective-permute-done.13), channel_id=1, source_target_pairs={{1,2},{2,3},{5,6},{6,7},{9,10},{10,11},{13,14},{14,15},{17,18},{18... | collective-permute-start | bytes 2359304 | tf_op jit(solution)/shard_map/ppermute | solution.py:20
  120.8 24.4 %collective-permute-start.19 = (f32[256,768]{0,1:T(8,128)}, f32[256,768]{0,1:T(8,128)}, u32[]{:S(2)}, u32[]{:S(2)}) collective-permute-start(f32[256,768]{0,1:T(8,128)} %collective-permute-done.14), channel_id=1, source_target_pairs={{1,0},{2,1},{5,4},{6,5},{9,8},{10,9},{13,12},{14,13},{17,16},{18,1... | collective-permute-start | bytes 2359304 | tf_op jit(solution)/shard_map/ppermute | solution.py:20
  131.3 8.5 %collective-permute-start.17 = (f32[8,32,256]{2,1,0:T(8,128)S(1)}, f32[8,32,256]{2,1,0:T(8,128)S(1)}, u32[]{:S(2)}, u32[]{:S(2)}) collective-permute-start(f32[8,32,256]{2,1,0:T(8,128)S(1)} %all-to-all-done.1), channel_id=1, source_target_pairs={{0,8},{8,0},{16,24},{24,16},{32,40},{40,32},{48,56},{56,48},{64,72... | collective-permute-start | bytes 786440 | tf_op jit(solution)/shard_map/ppermute | solution.py:28
  132.1 7.6 %collective-permute-start.20 = (f32[64,256]{1,0:T(8,128)S(1)}, f32[64,256]{1,0:T(8,128)S(1)}, u32[]{:S(2)}, u32[]{:S(2)}) collective-permute-start(f32[64,256]{1,0:T(8,128)S(1)} %get-tuple-element.88), channel_id=1, source_target_pairs={{0,4},{1,5},{2,6},{3,7},{4,0},{5,1},{6,2},{7,3},{8,12},{9,13},{10,... | collective-permute-start | bytes 196616 | tf_op jit(solution)/shard_map/ppermute | solution.py:147
  139.7 27.5 %copy-start.9 = (f32[2,64,256]{2,1,0:T(8,128)}, f32[2,64,256]{2,1,0:T(8,128)S(1)}, u32[]{:S(2)}) copy-start(f32[2,64,256]{2,1,0:T(8,128)S(1)} %maximum_select_fusion.6) | copy-start | bytes 393220
  145.3 29.9 %collective-permute-start.21 = (f32[256,768]{0,1:T(8,128)}, f32[256,768]{0,1:T(8,128)}, u32[]{:S(2)}, u32[]{:S(2)}) collective-permute-start(f32[256,768]{0,1:T(8,128)} %collective-permute-done.18), channel_id=1, source_target_pairs={{2,3},{6,7},{10,11},{14,15},{18,19},{22,23},{26,27},{30,31},{34,35... | collective-permute-start | bytes 2359304 | tf_op jit(solution)/shard_map/ppermute | solution.py:20
  146.8 28.4 %collective-permute-start.22 = (f32[256,768]{0,1:T(8,128)}, f32[256,768]{0,1:T(8,128)}, u32[]{:S(2)}, u32[]{:S(2)}) collective-permute-start(f32[256,768]{0,1:T(8,128)} %collective-permute-done.19), channel_id=1, source_target_pairs={{1,0},{5,4},{9,8},{13,12},{17,16},{21,20},{25,24},{29,28},{33,32},... | collective-permute-start | bytes 2359304 | tf_op jit(solution)/shard_map/ppermute | solution.py:20
  148.1 19.1 %collective-permute-start.25 = (f32[512,256]{1,0:T(8,128)}, f32[512,256]{1,0:T(8,128)}, u32[]{:S(2)}, u32[]{:S(2)}) collective-permute-start(f32[512,256]{1,0:T(8,128)} %get-tuple-element.61), channel_id=1, source_target_pairs={{0,8},{8,0},{16,24},{24,16},{32,40},{40,32},{48,56},{56,48},{64,72... | collective-permute-start | bytes 1572872 | tf_op jit(solution)/shard_map/ppermute | solution.py:28
  152.9 21.2 %all-to-all-start.2 = ((f32[16,16,512]{2,1,0:T(8,128)}), f32[16,16,512]{2,1,0:T(8,128)}, u32[]{:S(2)}, u32[]{:S(2)}) async-start(f32[16,16,512]{2,1,0:T(8,128)} %bitcast.61), calls=%async_computation.2 | async-start | bytes 1048576 | tf_op jit(solution)/shard_map/all_to_all | solution.py:166
  159.7 14.4 %collective-permute-start.23 = (f32[2,64,256]{2,1,0:T(8,128)S(1)}, f32[2,64,256]{2,1,0:T(8,128)S(1)}, u32[]{:S(2)}, u32[]{:S(2)}) collective-permute-start(f32[2,64,256]{2,1,0:T(8,128)S(1)} %maximum_select_fusion.6), channel_id=1, source_target_pairs={{0,1},{1,0},{2,3},{3,2},{4,5},{5,4},{6,7},{7,6},{8,9},{9,8},{10,11... | collective-permute-start | bytes 393224 | tf_op jit(solution)/shard_map/ppermute | solution.py:32
  167.2 6.9 %copy-start.10 = (f32[2,64,256]{2,1,0:T(8,128)S(1)}, f32[2,64,256]{2,1,0:T(8,128)}, u32[]{:S(2)}) copy-start(f32[2,64,256]{2,1,0:T(8,128)} %copy-done.9) | copy-start | bytes 393220
  180.7 24.7 %all-to-all-start.3 = ((f32[8,16,512]{2,1,0:T(8,128)}), f32[8,16,512]{2,1,0:T(8,128)}, u32[]{:S(2)}, u32[]{:S(2)}) async-start(f32[8,16,512]{2,1,0:T(8,128)} %broadcast_in_dim.11), calls=%async_computation.3 | async-start | bytes 524288 | tf_op jit(solution)/shard_map/all_to_all | solution.py:46
  184.8 19.2 %collective-permute-start.24 = (f32[2,2,64,256]{3,2,1,0:T(8,128)S(1)}, f32[2,2,64,256]{3,2,1,0:T(8,128)S(1)}, u32[]{:S(2)}, u32[]{:S(2)}) collective-permute-start(f32[2,2,64,256]{3,2,1,0:T(8,128)S(1)} %maximum_select_fusion.5), channel_id=1, source_target_pairs={{0,2},{1,3},{2,0},{3,1},{4,6},{5,7},{6,4},{7,5},{8,10},{9,11},{10,... | collective-permute-start | bytes 786440 | tf_op jit(solution)/shard_map/ppermute | solution.py:32
  187.0 3.7 %copy-start.16 = (f32[256,256]{1,0:T(8,128)S(1)}, f32[256,256]{1,0:T(8,128)}, u32[]{:S(2)}) copy-start(f32[256,256]{1,0:T(8,128)} %fusion.15) | copy-start | bytes 786436
  190.7 13.4 %copy-start.6 = (f32[256,768]{1,0:T(8,128)}, f32[256,768]{1,0:T(8,128)S(1)}, u32[]{:S(2)}) copy-start(f32[256,768]{1,0:T(8,128)S(1)} %fusion) | copy-start | bytes 2359300
  205.4 5.1 %copy-start.2 = (f32[1024,512]{1,0:T(8,128)S(1)}, f32[1024,512]{1,0:T(8,128)}, u32[]{:S(2)}) copy-start(f32[1024,512]{1,0:T(8,128)} %scatter_custom_fusion.1) | copy-start | bytes 6291460
  205.4 5.1 %copy-start.3 = (f32[1024,256]{1,0:T(8,128)S(1)}, f32[1024,256]{1,0:T(8,128)}, u32[]{:S(2)}) copy-start(f32[1024,256]{1,0:T(8,128)} %fusion.53) | copy-start | bytes 3145732
  205.4 4.0 %collective-permute-start.26 = (f32[8,16,512]{2,1,0:T(8,128)}, f32[8,16,512]{2,1,0:T(8,128)S(1)}, u32[]{:S(2)}, u32[]{:S(2)}) collective-permute-start(f32[8,16,512]{2,1,0:T(8,128)} %all-to-all-done.3), channel_id=1, source_target_pairs={{0,8},{8,0},{16,24},{24,16},{32,40},{40,32},{48,56},{56,48},{64,72... | collective-permute-start | bytes 786440 | tf_op jit(solution)/shard_map/ppermute | solution.py:28
  (1 other events, 1.2 us)
where the time goes:
time: 214 us; the launch traced here: 213 us
  starting transfers between devices  79.9 us (37%)
  waiting for transfers between devices  49.4 us (23%)
  matrix products  38.5 us (18%)
  local copies, waits for them, and re-layouts  28.6 us (13%)
  other arithmetic  12.8 us (6%)
  Pallas kernels  3.39 us (2%)
    dot_general x15, matrix products, dot(): lax.dot_general(left, right, (((left_dim,), (right_dim,)), ((), ())), pre...  38.5 us
    ppermute x12, starting transfers between devices, line_shift(): return lax.ppermute(value, ALL, pairs)  25.6 us
    ppermute x7, waiting for transfers between devices, ring_shift(): return lax.ppermute(value, 'gy', [(i, (i + step) % 8) for i in range(8)])  13.7 us
    ppermute x2, waiting for transfers between devices, join_partner(): other = lax.ppermute(value, 'gy', [(i, i ^ 1 << bit) for i in range(8)])  12.6 us
    scatter x2, local copies, waits for them, and re-layouts, per_device(): jnp.zeros_like(rows).at[order_row].set(rows, unique_indices=True)  12.5 us
    ppermute x7, starting transfers between devices, ring_shift(): return lax.ppermute(value, 'gy', [(i, (i + step) % 8) for i in range(8)])  12.4 us
    all_to_all x2, starting transfers between devices, node_gather(): lax.all_to_all(jnp.broadcast_to(block[None], (8,) + block.shape), 'gy', 0...  11.7 us
    all_to_all x1, starting transfers between devices, node_exchange(): return lax.all_to_all(pieces, ALL, 0, 0, axis_index_groups=groups)  9.48 us
  transfers between devices with their start and end apart: 31, of which 8 were waited for; matrix products, arithmetic and copies ran while one was open for 29% of the time, Pallas kernels for 2%

commit v1 on v0

--- a/solution.py
+++ b/solution.py
@@ -26,11 +26,6 @@
 
 def other_core(value):
     return lax.ppermute(value, "gx", [(i, i ^ 1) for i in range(32)])
-
-
-def join_partner(value, z, bit):
-    other = lax.ppermute(value, "gy", [(i, i ^ 1 << bit) for i in range(8)])
-    return jnp.where(z >> bit & 1 == 0, jnp.stack([value, other]), jnp.stack([other, value]))
 
 
 def node_exchange(pieces):
@@ -70,6 +65,13 @@
     )(z.reshape(1), *pieces)
 
 
+def inverse(order):
+    count = order.shape[0]
+    place = lax.broadcasted_iota(jnp.int32, (count, count), 1)
+    found = order[None, :] == lax.broadcasted_iota(jnp.int32, (count, count), 0)
+    return jnp.sum(jnp.where(found, place, 0), 1)
+
+
 def per_device(
     labels,
     point_order,
@@ -86,17 +88,17 @@
     order_row = point_order[0]
     barrier = lax.optimization_barrier
 
-    unorder = lambda rows: jnp.zeros_like(rows).at[order_row].set(rows, unique_indices=True)
-
     gains = dot(transfer_one, couple_one, 0, 0)
     ring = jnp.concatenate([couple_two, transfer_two], 1)
-    gain_right = line_shift(column(gains, child + 3), 1, (0,))
-    gain_left = line_shift(column(gains, child - 3), -1, (3,))
+    pairs = [(i, i + (1 if i & 3 == 0 else -1)) for i in range(256) if i & 3 in (0, 3)]
+    gain = lax.ppermute(column(gains, jnp.where(child == 0, 3, 0)), ALL, pairs)
     ring_right, ring_left = ring_shift(ring, 1), ring_shift(ring, -1)
     rhs = labels[order_row]
-    gain_right, gain_left, ring_right, ring_left, rhs = barrier(
-        (gain_right, gain_left, ring_right, ring_left, rhs)
+    inverse_order = inverse(order_row)
+    gain, ring_right, ring_left, rhs, inverse_order = barrier(
+        (gain, ring_right, ring_left, rhs, inverse_order)
     )
+    gain_right, gain_left = (jnp.where(child == 1, gain, 0.0), jnp.where(child == 2, gain, 0.0))
     rings = {0: ring, 1: ring_right, -1: ring_left}
 
     gain_right = line_shift(column(gains, child + 2) + gain_right, 1, (0, 1))
@@ -119,22 +121,14 @@
     rings |= {3: ring_right, -3: ring_left}
 
     ring_right = ring_shift(ring_right, 1)
-    gain_one = column(gains, child) + gain_right + gain_left
-    partial = dot(proj, gain_one, 0, 1)
+    partial = dot(proj, column(gains, child) + gain_right + gain_left, 0, 1)
     parts = node_exchange(partial.reshape(16, 32, 256))
     right_one = line_shift(block, 1, (0, 1, 2))
     left_one = line_shift(block, -1, (3, 2, 1))
     back = dot(leaf_inverse, leaf_basis)
-    back_out = unorder(back)
-    solved_out = unorder(solved)
-    parts, ring_right, right_one, left_one, back_out, solved_out = barrier(
-        (parts, ring_right, right_one, left_one, back_out, solved_out)
-    )
     rings |= {4: ring_right}
+    couple_core, transfer_core = place_rows([rings[s] for s in range(-3, 5)], z)
 
-    right_two = line_shift(right_one, 1, (1, 2))
-    left_two = line_shift(left_one, -1, (2, 1))
-    couple_core, transfer_core = place_rows([rings[s] for s in range(-3, 5)], z)
     stack_mine = parts.reshape(4, 4, 32, 256).sum(1)
     stack_other = other_core(stack_mine)
     stack_two = jnp.where(
@@ -144,40 +138,19 @@
     )
     stack_two = jnp.concatenate([stack_two[c] for c in range(4)], 1)
     solve_two = dot(stack_two, couple_core, 1, 1)
+    reduced = dot(solve_two, transfer_core)
+    reduced = lax.dynamic_slice(reduced, (core * 32, 0), (32, 256)) + other_core(
+        lax.dynamic_slice(reduced, ((1 - core) * 32, 0), (32, 256))
+    )
+    reduced_all = node_gather(reduced, core)
     far = lax.ppermute(
         jnp.where(half == 0, solve_two[:, 256:], solve_two[:, :256]),
         "gy",
         [(i, i ^ 4) for i in range(8)],
     )
-    near = jnp.where(half == 0, solve_two[:, :256], solve_two[:, 256:])
-    shares = jnp.where(half == 0, jnp.stack([near, far]), jnp.stack([far, near]))
-    reduced = dot(solve_two, transfer_core)
-    reduced = lax.dynamic_slice(reduced, (core * 32, 0), (32, 256)) + other_core(
-        lax.dynamic_slice(reduced, ((1 - core) * 32, 0), (32, 256))
-    )
-    reduced_all = node_gather(reduced, core)
-    reduced_all, right_two, left_two, shares = barrier((reduced_all, right_two, left_two, shares))
-
-    right_three = line_shift(right_two, 1, (2,))
-    left_three = line_shift(left_two, -1, (1,))
-    shares = join_partner(shares, z, 0)
-    top_partial = dot(couple_top, reduced_all, 1, 1).reshape(16, 16, 512)
-    planes = [[i for i in range(32) if i % 2 == k] for k in range(2)]
-    own_rows = lax.all_to_all(top_partial, "gx", 0, 0, axis_index_groups=planes).sum(0)
-    own_rows, right_three, left_three, shares = barrier(
-        (own_rows, right_three, left_three, shares)
-    )
-
-    shares = join_partner(shares, z, 1)
-    block_two = node_gather(own_rows, core)
-
-    couple_turned = jnp.concatenate([column(couple_one, child - s) for s in range(4)], 1)
-    stack_one = jnp.concatenate(
-        [block, right_one + left_three, right_two + left_two, right_three + left_one], 0
-    )
-    solve_lift = dot(couple_turned, stack_one)
-    solve_one, lift_one = solve_lift[:, :512], solve_lift[:, 512:]
-
+    right_two = line_shift(right_one, 1, (1, 2))
+    left_two = line_shift(left_one, -1, (2, 1))
+    back_out = back[inverse_order]
     transfer_other = other_core(transfer_core)
     transfer_all = jnp.where(
         core == 0,
@@ -185,13 +158,35 @@
         jnp.concatenate([transfer_other, transfer_core], 0),
     )
     lift_two = dot(lax.dynamic_slice(couple_core, (half * 256, 0), (256, 1024)), transfer_all)
+
+    top_partial = dot(couple_top, reduced_all, 1, 1).reshape(16, 16, 512)
+    planes = [[i for i in range(32) if i % 2 == k] for k in range(2)]
+    own_rows = lax.all_to_all(top_partial, "gx", 0, 0, axis_index_groups=planes)
+    near = jnp.where(half == 0, solve_two[:, :256], solve_two[:, 256:])
+    shares = jnp.where(half == 0, jnp.stack([near, far]), jnp.stack([far, near]))
+    far = lax.ppermute(shares, "gy", [(i, i ^ 2) for i in range(8)])
+    right_three = line_shift(right_two, 1, (2,))
+    left_three = line_shift(left_two, -1, (1,))
+    solved_out = solved[inverse_order]
+    couple_turned = jnp.concatenate([column(couple_one, child - s) for s in range(4)], 1)
+
+    block_two = node_gather(own_rows.sum(0), core)
+    shares = jnp.where(z & 2 == 0, jnp.stack([shares, far]), jnp.stack([far, shares]))
+    far = lax.ppermute(shares, "gy", [(i, i ^ 1) for i in range(8)])
+
+    stack_one = jnp.concatenate(
+        [block, right_one + left_three, right_two + left_two, right_three + left_one], 0
+    )
+    solve_lift = dot(couple_turned, stack_one)
+    solve_one, lift_one = solve_lift[:, :512], solve_lift[:, 512:]
     lift_both = dot(lift_one, lift_two)
     top_out = dot(back_out, lift_both)
-    shares = shares.reshape(2, 2, 2, 2, 32, 256).transpose(3, 2, 0, 1, 4, 5)
+    shares = jnp.where(z & 1 == 0, jnp.stack([shares, far]), jnp.stack([far, shares]))
+    shares = shares.reshape(2, 2, 2, 2, 32, 256).transpose(3, 2, 1, 0, 4, 5)
     solve_two_own = shares.reshape(512, 256)
     known = solve_one - dot(lift_one, solve_two_own, 1, 1)
-    base_out = solved_out - dot(back_out, known)
-    return base_out - dot(top_out, block_two)
+    both_out = jnp.concatenate([back_out, top_out], 1)
+    return solved_out - dot(both_out, jnp.concatenate([known, block_two], 0))
 
 
 def solution(mesh):

time: 214 us -> 194 us (0.907)
  waiting for transfers between devices: 49.4 us -> 27.3 us
  starting transfers between devices: 79.9 us -> 86.3 us
  matrix products: 38.5 us -> 32.3 us
    all_to_all x1, waiting for transfers between devices: 0.01 us -> 14.5 us  [node_exchange(): return lax.all_to_all(pieces, ALL, 0, 0, axis_index_groups=groups)]
    gather x0 -> x3, local copies, waits for them, and re-layouts: none -> 14.1 us  [the longest x2 7.24 us: per_device(): back_out = back[inverse_order]]
    scatter x2 -> x0, local copies, waits for them, and re-layouts: 12.5 us -> none  [per_device(): jnp.zeros_like(rows).at[order_row].set(rows, unique_indices=True)]
    ppermute x2 -> x3, waiting for transfers between devices: 12.6 us -> 2.13 us  [the longest x1 1.9 us: per_device(): far = lax.ppermute(shares, 'gy', [(i, i ^ 1) for i in range(8)])]
    ppermute x7, waiting for transfers between devices: 13.7 us -> 5.21 us  [ring_shift(): return lax.ppermute(value, 'gy', [(i, (i + step) % 8) for i in range(8)])]
    all_to_all x2, waiting for transfers between devices: 9.12 us -> 0.73 us  [node_gather(): lax.all_to_all(jnp.broadcast_to(block[None], (8,) + block.shape), 'gy', 0...]
    ppermute x1, waiting for transfers between devices: 7.27 us -> 0.01 us  [per_device(): lax.ppermute(jnp.where(half == 0, solve_two[:, 256:], solve_two[:, :256])...]
    ppermute x2 -> x3, starting transfers between devices: 7.58 us -> 14.3 us  [the longest x1 9.26 us: per_device(): far = lax.ppermute(shares, 'gy', [(i, i ^ 2) for i in range(8)])]
  transfers between devices with their start and end apart: 31 -> 30, of which waited for: 8 -> 6; matrix products, arithmetic and copies ran while one was open for 29% -> 33% of each run, Pallas kernels for 2% -> 2%
where the time goes in v1:
time: 194 us; the launch traced here: 192 us
  starting transfers between devices  86.3 us (44%)
  matrix products  32.3 us (17%)
  local copies, waits for them, and re-layouts  30.6 us (16%)
  waiting for transfers between devices  27.3 us (14%)
  other arithmetic  12 us (6%)
  Pallas kernels  3.38 us (2%)
    dot_general x14, matrix products, dot(): lax.dot_general(left, right, (((left_dim,), (right_dim,)), ((), ())), pre...  32.3 us
    ppermute x10, starting transfers between devices, line_shift(): return lax.ppermute(value, ALL, pairs)  23.4 us
    all_to_all x1, waiting for transfers between devices, node_exchange(): return lax.all_to_all(pieces, ALL, 0, 0, axis_index_groups=groups)  14.5 us
    ppermute x7, starting transfers between devices, ring_shift(): return lax.ppermute(value, 'gy', [(i, (i + step) % 8) for i in range(8)])  13.3 us
    all_to_all x1, starting transfers between devices, node_exchange(): return lax.all_to_all(pieces, ALL, 0, 0, axis_index_groups=groups)  9.48 us
    ppermute x1, starting transfers between devices, per_device(): far = lax.ppermute(shares, 'gy', [(i, i ^ 2) for i in range(8)])  9.26 us
    all_to_all x2, starting transfers between devices, node_gather(): lax.all_to_all(jnp.broadcast_to(block[None], (8,) + block.shape), 'gy', 0...  8.13 us
    gather x2, local copies, waits for them, and re-layouts, per_device(): back_out = back[inverse_order]  7.24 us
  transfers between devices with their start and end apart: 30, of which 6 were waited for; matrix products, arithmetic and copies ran while one was open for 33% of the time, Pallas kernels for 2%

profile of v1, /device:TPU:1, one launch (start us, length us, event | category | flops | bytes accessed | tf_op | source)
XLA Modules:
  0.0 192.4 jit_solution(16515448505171977398)
XLA Ops:
  2.0 6.4 %collective-permute-start.2 = (f32[64,1280]{1,0:T(8,128)S(1)}, f32[64,1280]{1,0:T(8,128)}, u32[]{:S(2)}, u32[]{:S(2)}) collective-permute-start(f32[64,1280]{1,0:T(8,128)S(1)} %constant_dynamic-update-slice_fusion.refs_3_), channel_id=1, source_target_pairs={{0,7},{1,0},{2,1},{3,2},{4,3},{5,4},{6,5},{7,6},{8,15},{9,8},{10,9... | collective-permute-start | bytes 983048 | tf_op jit(solution)/shard_map/ppermute | solution.py:24
  8.4 1.9 %fusion.56 = f32[256,1024]{1,0:T(8,128)S(1)} fusion(f32[256,256]{1,0:T(8,128)} %param.14, f32[256,1024]{1,0:T(8,128)} %param.13), kind=kOutput, calls=%fused_computation.96 | convolution fusion | flops 402653184 | bytes 2359296 | tf_op jit(solution)/shard_map/dot_general | solution.py:13
  11.1 2.0 %collective-permute-start = (f32[256,256]{1,0:T(8,128)}, f32[256,256]{1,0:T(8,128)}, u32[]{:S(2)}, u32[]{:S(2)}) collective-permute-start(f32[256,256]{1,0:T(8,128)} %constant_dynamic-slice_fusion.5), channel_id=1, source_target_pairs={{0,1},{3,2},{4,5},{7,6},{8,9},{11,10},{12,13},{15,14},{16,17},{19,... | collective-permute-start | bytes 786440 | tf_op jit(solution)/shard_map/ppermute | solution.py:94
  13.1 1.8 copy.23
  14.9 4.9 %gather_fusion = f32[1024,512]{1,0:T(8,128)} fusion(f32[1024,512]{1,0:T(8,128)S(1)} %copy-done, s32[1024]{0:T(1024)S(1)} %broadcast_clamp_fusion), kind=kCustom, calls=%fused_computation | custom fusion | bytes 4198400 | tf_op jit(solution)/shard_map/gather | solution.py:96
  22.2 4.7 %collective-permute-start.3 = (f32[256,256]{1,0:T(8,128)S(1)}, f32[256,256]{1,0:T(8,128)S(1)}, u32[]{:S(2)}, u32[]{:S(2)}) collective-permute-start(f32[256,256]{1,0:T(8,128)S(1)} %get-tuple-element.44), channel_id=1, source_target_pairs={{0,1},{1,2},{4,5},{5,6},{8,9},{9,10},{12,13},{13,14},{16,17},{17,1... | collective-permute-start | bytes 786440 | tf_op jit(solution)/shard_map/ppermute | solution.py:20
  27.0 2.1 %collective-permute-start.5 = (f32[64,1280]{1,0:T(8,128)}, f32[64,1280]{1,0:T(8,128)S(1)}, u32[]{:S(2)}, u32[]{:S(2)}) collective-permute-start(f32[64,1280]{1,0:T(8,128)} %collective-permute-done.1.refs_4_), channel_id=1, source_target_pairs={{0,1},{1,2},{2,3},{3,4},{4,5},{5,6},{6,7},{7,0},{8,9},{9,10},{10,1... | collective-permute-start | bytes 983048 | tf_op jit(solution)/shard_map/ppermute | solution.py:24
  29.7 9.4 %convolution_bitcast_fusion = f32[1024,512]{0,1:T(8,128)S(1)} fusion(f32[1024,512]{1,0:T(8,128)} %gather_fusion, f32[1024,1024]{1,0:T(8,128)} %param.11), kind=kOutput, calls=%fused_computation.17 | convolution fusion | flops 3221225472 | bytes 8388608 | tf_op jit(solution)/shard_map/dot_general | solution.py:13
  39.3 1.6 collective-permute-start.8
  40.9 4.0 %collective-permute-start.7 = (f32[256,256]{1,0:T(8,128)S(1)}, f32[256,256]{1,0:T(8,128)S(1)}, u32[]{:S(2)}, u32[]{:S(2)}) collective-permute-start(f32[256,256]{1,0:T(8,128)S(1)} %get-tuple-element.50), channel_id=1, source_target_pairs={{0,1},{1,2},{2,3},{4,5},{5,6},{6,7},{8,9},{9,10},{10,11},{12,13},{... | collective-permute-start | bytes 786440 | tf_op jit(solution)/shard_map/ppermute | solution.py:20
  44.9 1.4 collective-permute-start.9
  46.3 1.4 collective-permute-start.10
  49.7 5.2 %collective-permute-done.9.refs_6_ = f32[64,1280]{1,0:T(8,128)S(1)} collective-permute-done((f32[64,1280]{1,0:T(8,128)S(1)}, f32[64,1280]{1,0:T(8,128)S(1)}, u32[]{:S(2)}, u32[]{:S(2)}) %collective-permute-start.9) | collective-permute-done | bytes 327712 | tf_op jit(solution)/shard_map/ppermute | solution.py:24
  54.9 1.2 fusion.38
  56.2 9.5 %all-to-all-start = ((f32[16,32,256]{2,1,0:T(8,128)}), f32[16,32,256]{2,1,0:T(8,128)S(1)}, u32[]{:S(2)}, u32[]{:S(2)}) async-start(f32[16,32,256]{2,1,0:T(8,128)} %bitcast.70), calls=%async_computation | async-start | bytes 1048576 | tf_op jit(solution)/shard_map/all_to_all | solution.py:33
  65.7 1.4 collective-permute-start.17
  67.0 14.5 %all-to-all-done = f32[16,32,256]{2,1,0:T(8,128)S(1)} async-done(((f32[16,32,256]{2,1,0:T(8,128)}), f32[16,32,256]{2,1,0:T(8,128)S(1)}, u32[]{:S(2)}, u32[]{:S(2)}) %all-to-all-start) | async-done | bytes 524320 | tf_op jit(solution)/shard_map/all_to_all | solution.py:33
  81.8 1.3 collective-permute-start.12
  83.1 5.5 %collective-permute-start.11 = (f32[256,768]{0,1:T(8,128)}, f32[256,768]{0,1:T(8,128)}, u32[]{:S(2)}, u32[]{:S(2)}) collective-permute-start(f32[256,768]{0,1:T(8,128)} %pad_maximum_fusion), channel_id=1, source_target_pairs={{0,1},{1,2},{2,3},{4,5},{5,6},{6,7},{8,9},{9,10},{10,11},{12,13},{... | collective-permute-start | bytes 2359304 | tf_op jit(solution)/shard_map/ppermute | solution.py:20
  89.3 3.4 %shard_map.91 = (f32[512,1024]{1,0:T(8,128)}, f32[512,256]{1,0:T(8,128)}) custom-call(s32[1]{0:T(128)} %bitcast.5.z_ref, f32[64,1280]{1,0:T(8,128)} %copy-done.16, f32[64,1280]{1,0:T(8,128)} %copy-done.14, f32[64,1280]{1,0:T(8,128)} %collective-permute-done.2.refs_2_, f32[64,1280]{1,0:T(8,128)} %copy-done.8, f32[64,1280]{1,0:T(8,128)} %collective-permute-done.1.refs_4_, ...), custom_call_target="tpu_custom_call" | custom-call | tf_op jit(solution)/shard_map/pallas_call | solution.py:56
  92.7 2.8 %fusion.30 = f32[64,512]{1,0:T(8,128)S(1)} fusion(f32[512,1024]{1,0:T(8,128)} %get-tuple-element.38, f32[64,256]{1,0:T(8,128)S(1)} %get-tuple-element.52, f32[64,256]{1,0:T(8,128)S(1)} %get-tuple-element.53, f32[64,256]{1,0:T(8,128)S(1)} %get-tuple-element.54, f32[64,256]{1,0:T(8,128)S(1)} %get-tuple-element.51), kind=kOutput, calls=%fused_computation.45 | convolution fusion | flops 201523200 | bytes 2490368 | tf_op jit(solution)/shard_map/dot_general | solution.py:13
  95.5 1.3 fusion.59
  99.0 4.0 %all-to-all-start.1 = ((f32[8,32,256]{2,1,0:T(8,128)}), f32[8,32,256]{2,1,0:T(8,128)S(1)}, u32[]{:S(2)}, u32[]{:S(2)}) async-start(f32[8,32,256]{2,1,0:T(8,128)} %broadcast_in_dim.29), calls=%async_computation.1 | async-start | bytes 524288 | tf_op jit(solution)/shard_map/all_to_all | solution.py:41
  103.0 2.9 %copy.22 = f32[1024,512]{1,0:T(8,128)} copy(f32[1024,512]{0,1:T(8,128)} %copy-done.1) | data formatting | bytes 4194304 | tf_op jit(solution)/shard_map/optimization_barrier | solution.py:108
  105.9 6.9 %gather_fusion.1 = f32[1024,512]{1,0:T(8,128)} fusion(f32[1024,512]{1,0:T(8,128)} %copy.22, s32[1024]{0:T(1024)S(1)} %fusion.49), kind=kCustom, calls=%fused_computation.1 | custom fusion | bytes 4198400 | tf_op jit(solution)/shard_map/gather | solution.py:170
  113.2 1.3 collective-permute-start.13
  114.5 1.6 collective-permute-start.15
  116.1 4.3 %fusion.57 = f32[1024,256]{1,0:T(8,128)S(1)} fusion(f32[1024,1024]{1,0:T(8,128)} %param.11, f32[1024,256]{1,0:T(8,128)} %param.12), kind=kOutput, calls=%fused_computation.97 | convolution fusion | flops 1610612736 | bytes 6291456 | tf_op jit(solution)/shard_map/dot_general | solution.py:13
  120.4 4.7 %gather_fusion.2 = f32[1024,256]{1,0:T(8,128)} fusion(f32[1024,256]{1,0:T(8,128)S(1)} %fusion.57, s32[1024]{0:T(1024)S(1)} %fusion.49), kind=kCustom, calls=%fused_computation.2 | custom fusion | bytes 2101248 | tf_op jit(solution)/shard_map/gather | solution.py:153
  125.1 2.5 %copy.24 = f32[1024,256]{0,1:T(8,128)} copy(f32[1024,256]{1,0:T(8,128)} %gather_fusion.2) | data formatting | bytes 2097152 | tf_op jit(solution)/shard_map/gather | solution.py:153
  127.7 5.7 %collective-permute-start.20 = (f32[64,256]{1,0:T(8,128)S(1)}, f32[64,256]{1,0:T(8,128)S(1)}, u32[]{:S(2)}, u32[]{:S(2)}) collective-permute-start(f32[64,256]{1,0:T(8,128)S(1)} %get-tuple-element.56), channel_id=1, source_target_pairs={{0,4},{1,5},{2,6},{3,7},{4,0},{5,1},{6,2},{7,3},{8,12},{9,13},{10,... | collective-permute-start | bytes 196616 | tf_op jit(solution)/shard_map/ppermute | solution.py:146
  133.4 3.2 %fusion.19 = f32[256,256]{1,0:T(8,128)} fusion(f32[512,256]{1,0:T(8,128)} %collective-permute-done.18, f32[512,256]{1,0:T(8,128)} %get-tuple-element.39, f32[512,1024]{1,0:T(8,128)} %get-tuple-element.38, s32[]{:T(128)S(6)} %select_n.199, pred[]{:T(512)S(6)} %eq.42), kind=kOutput, calls=%fused_computation.27 | convolution fusion | flops 403439616 | bytes 2359301 | tf_op jit(solution)/shard_map/dot_general | solution.py:13
  136.6 9.3 %collective-permute-start.21 = (f32[2,64,256]{2,1,0:T(8,128)S(1)}, f32[2,64,256]{2,1,0:T(8,128)S(1)}, u32[]{:S(2)}, u32[]{:S(2)}) collective-permute-start(f32[2,64,256]{2,1,0:T(8,128)S(1)} %maximum_select_fusion.9), channel_id=1, source_target_pairs={{0,2},{1,3},{2,0},{3,1},{4,6},{5,7},{6,4},{7,5},{8,10},{9,11},{10,... | collective-permute-start | bytes 393224 | tf_op jit(solution)/shard_map/ppermute | solution.py:167
  145.9 1.3 collective-permute-start.14
  147.2 1.6 collective-permute-start.16
  150.0 7.0 %all-to-all-start.2 = ((f32[16,16,512]{2,1,0:T(8,128)}), f32[16,16,512]{2,1,0:T(8,128)S(1)}, u32[]{:S(2)}, u32[]{:S(2)}) async-start(f32[16,16,512]{2,1,0:T(8,128)} %bitcast.32), calls=%async_computation.2 | async-start | bytes 1048576 | tf_op jit(solution)/shard_map/all_to_all | solution.py:164
  157.1 3.1 %collective-permute-start.22 = (f32[2,2,64,256]{3,2,1,0:T(8,128)S(1)}, f32[2,2,64,256]{3,2,1,0:T(8,128)S(1)}, u32[]{:S(2)}, u32[]{:S(2)}) collective-permute-start(f32[2,2,64,256]{3,2,1,0:T(8,128)S(1)} %maximum_select_fusion.7), channel_id=1, source_target_pairs={{0,1},{1,0},{2,3},{3,2},{4,5},{5,4},{6,7},{7,6},{8,9},{9,8},{10,11... | collective-permute-start | bytes 786440 | tf_op jit(solution)/shard_map/ppermute | solution.py:175
  160.2 2.4 %add.102 = f32[256,768]{0,1:T(8,128)} add(f32[256,768]{0,1:T(8,128)} %collective-permute-done.15, f32[256,768]{0,1:T(8,128)} %collective-permute-done.13) | non-fusion elementwise | flops 196608 | bytes 2359296 | tf_op jit(solution)/shard_map/add | solution.py:178
  162.5 4.6 %all-to-all-done.2 = f32[16,16,512]{2,1,0:T(8,128)S(1)} async-done(((f32[16,16,512]{2,1,0:T(8,128)}), f32[16,16,512]{2,1,0:T(8,128)S(1)}, u32[]{:S(2)}, u32[]{:S(2)}) %all-to-all-start.2) | async-done | bytes 524320 | tf_op jit(solution)/shard_map/all_to_all | solution.py:164
  167.9 4.2 %all-to-all-start.3 = ((f32[8,16,512]{2,1,0:T(8,128)}), f32[8,16,512]{2,1,0:T(8,128)}, u32[]{:S(2)}, u32[]{:S(2)}) async-start(f32[8,16,512]{2,1,0:T(8,128)} %broadcast_in_dim.30), calls=%async_computation.3 | async-start | bytes 524288 | tf_op jit(solution)/shard_map/all_to_all | solution.py:41
  172.1 1.9 collective-permute-done.22
  174.9 1.6 add.101
  176.5 1.5 add.103
  178.1 1.6 fusion
  181.6 3.8 %collective-permute-start.25 = (f32[8,16,512]{2,1,0:T(8,128)}, f32[8,16,512]{2,1,0:T(8,128)S(1)}, u32[]{:S(2)}, u32[]{:S(2)}) collective-permute-start(f32[8,16,512]{2,1,0:T(8,128)} %all-to-all-done.3), channel_id=1, source_target_pairs={{0,8},{8,0},{16,24},{24,16},{32,40},{40,32},{48,56},{56,48},{64,72... | collective-permute-start | bytes 786440 | tf_op jit(solution)/shard_map/ppermute | solution.py:28
  186.1 1.6 slice_subtract_fusion
  188.8 1.9 fusion.8
  190.6 1.8 sub.25
  (115 shorter events, 18.3 us)
Async XLA Ops:
  0.0 14.9 %copy-start = (f32[1024,512]{1,0:T(8,128)S(1)}, f32[1024,512]{1,0:T(8,128)}, u32[]{:S(2)}) copy-start(f32[1024,512]{1,0:T(8,128)} %param.9) | copy-start | bytes 6291460
  0.0 13.1 %copy-start.24 = (s32[1,1024]{1,0:T(1,128)S(1)}, s32[1,1024]{1,0:T(1,128)}, u32[]{:S(2)}) copy-start(s32[1,1024]{1,0:T(1,128)} %param.10) | copy-start | bytes 12292
  2.0 17.8 %copy-start.8 = (f32[64,1280]{1,0:T(8,128)}, f32[64,1280]{1,0:T(8,128)S(1)}, u32[]{:S(2)}) copy-start(f32[64,1280]{1,0:T(8,128)S(1)} %constant_dynamic-update-slice_fusion.refs_3_) | copy-start | bytes 983044
  2.0 18.5 %collective-permute-start.2 = (f32[64,1280]{1,0:T(8,128)S(1)}, f32[64,1280]{1,0:T(8,128)}, u32[]{:S(2)}, u32[]{:S(2)}) collective-permute-start(f32[64,1280]{1,0:T(8,128)S(1)} %constant_dynamic-update-slice_fusion.refs_3_), channel_id=1, source_target_pairs={{0,7},{1,0},{2,1},{3,2},{4,3},{5,4},{6,5},{7,6},{8,15},{9,8},{10,9... | collective-permute-start | bytes 983048 | tf_op jit(solution)/shard_map/ppermute | solution.py:24
  8.4 12.1 %collective-permute-start.1 = (f32[64,1280]{1,0:T(8,128)S(1)}, f32[64,1280]{1,0:T(8,128)}, u32[]{:S(2)}, u32[]{:S(2)}) collective-permute-start(f32[64,1280]{1,0:T(8,128)S(1)} %constant_dynamic-update-slice_fusion.refs_3_), channel_id=1, source_target_pairs={{0,1},{1,2},{2,3},{3,4},{4,5},{5,6},{6,7},{7,0},{8,9},{9,10},{10,1... | collective-permute-start | bytes 983048 | tf_op jit(solution)/shard_map/ppermute | solution.py:24
  11.1 9.4 %collective-permute-start = (f32[256,256]{1,0:T(8,128)}, f32[256,256]{1,0:T(8,128)}, u32[]{:S(2)}, u32[]{:S(2)}) collective-permute-start(f32[256,256]{1,0:T(8,128)} %constant_dynamic-slice_fusion.5), channel_id=1, source_target_pairs={{0,1},{3,2},{4,5},{7,6},{8,9},{11,10},{12,13},{15,14},{16,17},{19,... | collective-permute-start | bytes 786440 | tf_op jit(solution)/shard_map/ppermute | solution.py:94
  21.5 17.6 %collective-permute-start.4 = (f32[256,256]{1,0:T(8,128)S(1)}, f32[256,256]{1,0:T(8,128)S(1)}, u32[]{:S(2)}, u32[]{:S(2)}) collective-permute-start(f32[256,256]{1,0:T(8,128)S(1)} %get-tuple-element.43), channel_id=1, source_target_pairs={{2,1},{3,2},{6,5},{7,6},{10,9},{11,10},{14,13},{15,14},{18,17},{19... | collective-permute-start | bytes 786440 | tf_op jit(solution)/shard_map/ppermute | solution.py:20
  22.2 17.0 %collective-permute-start.3 = (f32[256,256]{1,0:T(8,128)S(1)}, f32[256,256]{1,0:T(8,128)S(1)}, u32[]{:S(2)}, u32[]{:S(2)}) collective-permute-start(f32[256,256]{1,0:T(8,128)S(1)} %get-tuple-element.44), channel_id=1, source_target_pairs={{0,1},{1,2},{4,5},{5,6},{8,9},{9,10},{12,13},{13,14},{16,17},{17,1... | collective-permute-start | bytes 786440 | tf_op jit(solution)/shard_map/ppermute | solution.py:20
  27.0 12.2 %collective-permute-start.5 = (f32[64,1280]{1,0:T(8,128)}, f32[64,1280]{1,0:T(8,128)S(1)}, u32[]{:S(2)}, u32[]{:S(2)}) collective-permute-start(f32[64,1280]{1,0:T(8,128)} %collective-permute-done.1.refs_4_), channel_id=1, source_target_pairs={{0,1},{1,2},{2,3},{3,4},{4,5},{5,6},{6,7},{7,0},{8,9},{9,10},{10,1... | collective-permute-start | bytes 983048 | tf_op jit(solution)/shard_map/ppermute | solution.py:24
  29.1 10.1 %collective-permute-start.6 = (f32[64,1280]{1,0:T(8,128)}, f32[64,1280]{1,0:T(8,128)S(1)}, u32[]{:S(2)}, u32[]{:S(2)}) collective-permute-start(f32[64,1280]{1,0:T(8,128)} %collective-permute-done.2.refs_2_), channel_id=1, source_target_pairs={{0,7},{1,0},{2,1},{3,2},{4,3},{5,4},{6,5},{7,6},{8,15},{9,8},{10,9... | collective-permute-start | bytes 983048 | tf_op jit(solution)/shard_map/ppermute | solution.py:24
  39.1 9.6 %copy-start.1 = (f32[1024,512]{0,1:T(8,128)}, f32[1024,512]{0,1:T(8,128)S(1)}, u32[]{:S(2)}) copy-start(f32[1024,512]{0,1:T(8,128)S(1)} %convolution_bitcast_fusion) | copy-start | bytes 6291460
  39.2 8.5 %copy-start.6 = (f32[1024,256]{1,0:T(8,128)S(1)}, f32[1024,256]{1,0:T(8,128)}, u32[]{:S(2)}) copy-start(f32[1024,256]{1,0:T(8,128)} %param.12) | copy-start | bytes 3145732
  39.2 9.5 %copy-start.13 = (f32[64,1280]{1,0:T(8,128)}, f32[64,1280]{1,0:T(8,128)S(1)}, u32[]{:S(2)}) copy-start(f32[64,1280]{1,0:T(8,128)S(1)} %collective-permute-done.5.refs_5_) | copy-start | bytes 983044
  39.2 9.5 %copy-start.14 = (f32[64,1280]{1,0:T(8,128)}, f32[64,1280]{1,0:T(8,128)S(1)}, u32[]{:S(2)}) copy-start(f32[64,1280]{1,0:T(8,128)S(1)} %collective-permute-done.6.refs_1_) | copy-start | bytes 983044
  39.3 9.4 %copy-start.9 = (f32[256,256]{0,1:T(8,128)S(1)}, f32[256,256]{0,1:T(8,128)}, u32[]{:S(2)}) copy-start(f32[256,256]{0,1:T(8,128)} %copy.23) | copy-start | bytes 786436
  39.3 10.4 %collective-permute-start.8 = (f32[256,256]{1,0:T(8,128)S(1)}, f32[256,256]{1,0:T(8,128)S(1)}, u32[]{:S(2)}, u32[]{:S(2)}) collective-permute-start(f32[256,256]{1,0:T(8,128)S(1)} %get-tuple-element.49), channel_id=1, source_target_pairs={{1,0},{2,1},{3,2},{5,4},{6,5},{7,6},{9,8},{10,9},{11,10},{13,12},{... | collective-permute-start | bytes 786440 | tf_op jit(solution)/shard_map/ppermute | solution.py:20
  40.9 8.8 %collective-permute-start.7 = (f32[256,256]{1,0:T(8,128)S(1)}, f32[256,256]{1,0:T(8,128)S(1)}, u32[]{:S(2)}, u32[]{:S(2)}) collective-permute-start(f32[256,256]{1,0:T(8,128)S(1)} %get-tuple-element.50), channel_id=1, source_target_pairs={{0,1},{1,2},{2,3},{4,5},{5,6},{6,7},{8,9},{9,10},{10,11},{12,13},{... | collective-permute-start | bytes 786440 | tf_op jit(solution)/shard_map/ppermute | solution.py:20
  44.9 10.0 %collective-permute-start.9 = (f32[64,1280]{1,0:T(8,128)S(1)}, f32[64,1280]{1,0:T(8,128)S(1)}, u32[]{:S(2)}, u32[]{:S(2)}) collective-permute-start(f32[64,1280]{1,0:T(8,128)S(1)} %collective-permute-done.5.refs_5_), channel_id=1, source_target_pairs={{0,1},{1,2},{2,3},{3,4},{4,5},{5,6},{6,7},{7,0},{8,9},{9,10},{10,1... | collective-permute-start | bytes 983048 | tf_op jit(solution)/shard_map/ppermute | solution.py:24
  46.3 8.6 %collective-permute-start.10 = (f32[64,1280]{1,0:T(8,128)S(1)}, f32[64,1280]{1,0:T(8,128)S(1)}, u32[]{:S(2)}, u32[]{:S(2)}) collective-permute-start(f32[64,1280]{1,0:T(8,128)S(1)} %collective-permute-done.6.refs_1_), channel_id=1, source_target_pairs={{0,7},{1,0},{2,1},{3,2},{4,3},{5,4},{6,5},{7,6},{8,15},{9,8},{10,9... | collective-permute-start | bytes 983048 | tf_op jit(solution)/shard_map/ppermute | solution.py:24
  56.2 25.3 %all-to-all-start = ((f32[16,32,256]{2,1,0:T(8,128)}), f32[16,32,256]{2,1,0:T(8,128)S(1)}, u32[]{:S(2)}, u32[]{:S(2)}) async-start(f32[16,32,256]{2,1,0:T(8,128)} %bitcast.70), calls=%async_computation | async-start | bytes 1048576 | tf_op jit(solution)/shard_map/all_to_all | solution.py:33
  65.7 22.9 %collective-permute-start.17 = (f32[64,1280]{1,0:T(8,128)}, f32[64,1280]{1,0:T(8,128)S(1)}, u32[]{:S(2)}, u32[]{:S(2)}) collective-permute-start(f32[64,1280]{1,0:T(8,128)} %copy-done.15), channel_id=1, source_target_pairs={{0,1},{1,2},{2,3},{3,4},{4,5},{5,6},{6,7},{7,0},{8,9},{9,10},{10,1... | collective-permute-start | bytes 983048 | tf_op jit(solution)/shard_map/ppermute | solution.py:24
  81.6 11.1 %collective-permute-start.19 = (f32[4,32,256]{2,1,0:T(8,128)S(1)}, f32[4,32,256]{2,1,0:T(8,128)S(1)}, u32[]{:S(2)}, u32[]{:S(2)}) collective-permute-start(f32[4,32,256]{2,1,0:T(8,128)S(1)} %bitcast_reduce_fusion), channel_id=1, source_target_pairs={{0,8},{8,0},{16,24},{24,16},{32,40},{40,32},{48,56},{56,48},{64,72... | collective-permute-start | bytes 393224 | tf_op jit(solution)/shard_map/ppermute | solution.py:28
  81.8 31.5 %collective-permute-start.12 = (f32[256,768]{0,1:T(8,128)}, f32[256,768]{0,1:T(8,128)}, u32[]{:S(2)}, u32[]{:S(2)}) collective-permute-start(f32[256,768]{0,1:T(8,128)} %pad_maximum_fusion), channel_id=1, source_target_pairs={{1,0},{2,1},{3,2},{5,4},{6,5},{7,6},{9,8},{10,9},{11,10},{13,12},{... | collective-permute-start | bytes 2359304 | tf_op jit(solution)/shard_map/ppermute | solution.py:20
  83.1 31.5 %collective-permute-start.11 = (f32[256,768]{0,1:T(8,128)}, f32[256,768]{0,1:T(8,128)}, u32[]{:S(2)}, u32[]{:S(2)}) collective-permute-start(f32[256,768]{0,1:T(8,128)} %pad_maximum_fusion), channel_id=1, source_target_pairs={{0,1},{1,2},{2,3},{4,5},{5,6},{6,7},{8,9},{9,10},{10,11},{12,13},{... | collective-permute-start | bytes 2359304 | tf_op jit(solution)/shard_map/ppermute | solution.py:20
  92.7 4.6 %copy-start.5 = (f32[256,1024]{1,0:T(8,128)S(1)}, f32[256,1024]{1,0:T(8,128)}, u32[]{:S(2)}) copy-start(f32[256,1024]{1,0:T(8,128)} %param.13) | copy-start | bytes 3145732
  96.8 1.4 collective-permute-start.23
  99.0 28.6 %all-to-all-start.1 = ((f32[8,32,256]{2,1,0:T(8,128)}), f32[8,32,256]{2,1,0:T(8,128)S(1)}, u32[]{:S(2)}, u32[]{:S(2)}) async-start(f32[8,32,256]{2,1,0:T(8,128)} %broadcast_in_dim.29), calls=%async_computation.1 | async-start | bytes 524288 | tf_op jit(solution)/shard_map/all_to_all | solution.py:41
  112.8 20.6 %collective-permute-start.18 = (f32[512,256]{1,0:T(8,128)}, f32[512,256]{1,0:T(8,128)}, u32[]{:S(2)}, u32[]{:S(2)}) collective-permute-start(f32[512,256]{1,0:T(8,128)} %get-tuple-element.39), channel_id=1, source_target_pairs={{0,8},{8,0},{16,24},{24,16},{32,40},{40,32},{48,56},{56,48},{64,72... | collective-permute-start | bytes 1572872 | tf_op jit(solution)/shard_map/ppermute | solution.py:28
  113.2 32.6 %collective-permute-start.13 = (f32[256,768]{0,1:T(8,128)}, f32[256,768]{0,1:T(8,128)}, u32[]{:S(2)}, u32[]{:S(2)}) collective-permute-start(f32[256,768]{0,1:T(8,128)} %collective-permute-done.12), channel_id=1, source_target_pairs={{1,0},{2,1},{5,4},{6,5},{9,8},{10,9},{13,12},{14,13},{17,16},{18,1... | collective-permute-start | bytes 2359304 | tf_op jit(solution)/shard_map/ppermute | solution.py:20
  114.5 32.6 %collective-permute-start.15 = (f32[256,768]{0,1:T(8,128)}, f32[256,768]{0,1:T(8,128)}, u32[]{:S(2)}, u32[]{:S(2)}) collective-permute-start(f32[256,768]{0,1:T(8,128)} %collective-permute-done.11), channel_id=1, source_target_pairs={{1,2},{2,3},{5,6},{6,7},{9,10},{10,11},{13,14},{14,15},{17,18},{18... | collective-permute-start | bytes 2359304 | tf_op jit(solution)/shard_map/ppermute | solution.py:20
  127.6 21.1 %copy-start.18 = (f32[256,256]{1,0:T(8,128)S(1)}, f32[256,256]{1,0:T(8,128)}, u32[]{:S(2)}) copy-start(f32[256,256]{1,0:T(8,128)} %param.17) | copy-start | bytes 786436
  127.6 21.1 %collective-permute-start.24 = (f32[8,32,256]{2,1,0:T(8,128)S(1)}, f32[8,32,256]{2,1,0:T(8,128)S(1)}, u32[]{:S(2)}, u32[]{:S(2)}) collective-permute-start(f32[8,32,256]{2,1,0:T(8,128)S(1)} %all-to-all-done.1), channel_id=1, source_target_pairs={{0,8},{8,0},{16,24},{24,16},{32,40},{40,32},{48,56},{56,48},{64,72... | collective-permute-start | bytes 786440 | tf_op jit(solution)/shard_map/ppermute | solution.py:28
  127.7 8.9 %collective-permute-start.20 = (f32[64,256]{1,0:T(8,128)S(1)}, f32[64,256]{1,0:T(8,128)S(1)}, u32[]{:S(2)}, u32[]{:S(2)}) collective-permute-start(f32[64,256]{1,0:T(8,128)S(1)} %get-tuple-element.56), channel_id=1, source_target_pairs={{0,4},{1,5},{2,6},{3,7},{4,0},{5,1},{6,2},{7,3},{8,12},{9,13},{10,... | collective-permute-start | bytes 196616 | tf_op jit(solution)/shard_map/ppermute | solution.py:146
  136.6 20.4 %collective-permute-start.21 = (f32[2,64,256]{2,1,0:T(8,128)S(1)}, f32[2,64,256]{2,1,0:T(8,128)S(1)}, u32[]{:S(2)}, u32[]{:S(2)}) collective-permute-start(f32[2,64,256]{2,1,0:T(8,128)S(1)} %maximum_select_fusion.9), channel_id=1, source_target_pairs={{0,2},{1,3},{2,0},{3,1},{4,6},{5,7},{6,4},{7,5},{8,10},{9,11},{10,... | collective-permute-start | bytes 393224 | tf_op jit(solution)/shard_map/ppermute | solution.py:167
  145.9 29.0 %collective-permute-start.14 = (f32[256,768]{0,1:T(8,128)}, f32[256,768]{0,1:T(8,128)}, u32[]{:S(2)}, u32[]{:S(2)}) collective-permute-start(f32[256,768]{0,1:T(8,128)} %collective-permute-done.13), channel_id=1, source_target_pairs={{1,0},{5,4},{9,8},{13,12},{17,16},{21,20},{25,24},{29,28},{33,32},... | collective-permute-start | bytes 2359304 | tf_op jit(solution)/shard_map/ppermute | solution.py:20
  147.2 29.3 %collective-permute-start.16 = (f32[256,768]{0,1:T(8,128)}, f32[256,768]{0,1:T(8,128)}, u32[]{:S(2)}, u32[]{:S(2)}) collective-permute-start(f32[256,768]{0,1:T(8,128)} %collective-permute-done.15), channel_id=1, source_target_pairs={{2,3},{6,7},{10,11},{14,15},{18,19},{22,23},{26,27},{30,31},{34,35... | collective-permute-start | bytes 2359304 | tf_op jit(solution)/shard_map/ppermute | solution.py:20
  150.0 17.1 %all-to-all-start.2 = ((f32[16,16,512]{2,1,0:T(8,128)}), f32[16,16,512]{2,1,0:T(8,128)S(1)}, u32[]{:S(2)}, u32[]{:S(2)}) async-start(f32[16,16,512]{2,1,0:T(8,128)} %bitcast.32), calls=%async_computation.2 | async-start | bytes 1048576 | tf_op jit(solution)/shard_map/all_to_all | solution.py:164
  157.1 16.9 %collective-permute-start.22 = (f32[2,2,64,256]{3,2,1,0:T(8,128)S(1)}, f32[2,2,64,256]{3,2,1,0:T(8,128)S(1)}, u32[]{:S(2)}, u32[]{:S(2)}) collective-permute-start(f32[2,2,64,256]{3,2,1,0:T(8,128)S(1)} %maximum_select_fusion.7), channel_id=1, source_target_pairs={{0,1},{1,0},{2,3},{3,2},{4,5},{5,4},{6,7},{7,6},{8,9},{9,8},{10,11... | collective-permute-start | bytes 786440 | tf_op jit(solution)/shard_map/ppermute | solution.py:175
  167.9 13.7 %all-to-all-start.3 = ((f32[8,16,512]{2,1,0:T(8,128)}), f32[8,16,512]{2,1,0:T(8,128)}, u32[]{:S(2)}, u32[]{:S(2)}) async-start(f32[8,16,512]{2,1,0:T(8,128)} %broadcast_in_dim.30), calls=%async_computation.3 | async-start | bytes 524288 | tf_op jit(solution)/shard_map/all_to_all | solution.py:41
  174.8 3.2 %copy-start.11 = (f32[256,768]{0,1:T(8,128)S(1)}, f32[256,768]{0,1:T(8,128)}, u32[]{:S(2)}) copy-start(f32[256,768]{0,1:T(8,128)} %add.102) | copy-start | bytes 2359300
  174.8 3.2 %copy-start.19 = (f32[256,256]{1,0:T(8,128)S(1)}, f32[256,256]{1,0:T(8,128)}, u32[]{:S(2)}) copy-start(f32[256,256]{1,0:T(8,128)} %get-tuple-element.45) | copy-start | bytes 786436
  174.8 3.2 %copy-start.20 = (f32[256,256]{1,0:T(8,128)S(1)}, f32[256,256]{1,0:T(8,128)}, u32[]{:S(2)}) copy-start(f32[256,256]{1,0:T(8,128)} %get-tuple-element.46) | copy-start | bytes 786436
  174.8 3.2 %copy-start.21 = (f32[256,256]{1,0:T(8,128)S(1)}, f32[256,256]{1,0:T(8,128)}, u32[]{:S(2)}) copy-start(f32[256,256]{1,0:T(8,128)} %get-tuple-element.47) | copy-start | bytes 786436
  174.8 3.2 %copy-start.22 = (f32[256,256]{1,0:T(8,128)S(1)}, f32[256,256]{1,0:T(8,128)}, u32[]{:S(2)}) copy-start(f32[256,256]{1,0:T(8,128)} %get-tuple-element.48) | copy-start | bytes 786436
  178.1 7.4 %copy-start.2 = (f32[1024,256]{1,0:T(8,128)S(1)}, f32[1024,256]{1,0:T(8,128)}, u32[]{:S(2)}) copy-start(f32[1024,256]{1,0:T(8,128)} %gather_fusion.2) | copy-start | bytes 3145732
  181.6 4.4 %copy-start.7 = (f32[2,2,2,2,32,256]{5,4,0,1,2,3:T(8,128)S(1)}, f32[2,2,2,2,32,256]{5,4,0,1,2,3:T(8,128)}, u32[]{:S(2)}) copy-start(f32[2,2,2,2,32,256]{5,4,0,1,2,3:T(8,128)} %maximum_select_fusion.2) | copy-start | bytes 1572868
  181.6 7.1 %copy-start.4 = (f32[1024,256]{0,1:T(8,128)S(1)}, f32[1024,256]{0,1:T(8,128)}, u32[]{:S(2)}) copy-start(f32[1024,256]{0,1:T(8,128)} %copy.24) | copy-start | bytes 3145732
  181.6 6.0 %collective-permute-start.25 = (f32[8,16,512]{2,1,0:T(8,128)}, f32[8,16,512]{2,1,0:T(8,128)S(1)}, u32[]{:S(2)}, u32[]{:S(2)}) collective-permute-start(f32[8,16,512]{2,1,0:T(8,128)} %all-to-all-done.3), channel_id=1, source_target_pairs={{0,8},{8,0},{16,24},{24,16},{32,40},{40,32},{48,56},{56,48},{64,72... | collective-permute-start | bytes 786440 | tf_op jit(solution)/shard_map/ppermute | solution.py:28
  (7 other events, 11.7 us)
